TPU v7x, 256 devices: a whole 4x4x8 slice. The times are simulated.
256 devices in a mesh: sector: 32 (over x, z), chan: 8 (over y, core).
Axes of the slice: x: 4, y: 4, z: 8, core: 2. Of those that a mesh axis runs over, the one named last changes fastest.
Arguments:
- environment: bfloat16 [4096, 16, 640], P('sector', 'chan'), may hold values from -6 to 6
- sector_sizes: int32 [16], replicated, may hold values from 128 to 640, as said below
- joining_table: int32 [2, 2, 16], replicated, may hold values from 0 to 15, as said below
- isometry: bfloat16 [2, 2, 640, 4096], P(None, None, None, 'sector'), may hold values from -1 to 1
- mixing: float32 [2, 2, 16, 16], replicated, may hold values from -1 to 1
Outputs:
- environment_out: bfloat16 [4096, 16, 640], P('sector', 'chan')
Inputs may be any that keep to these rules, and one draw needn't show every extreme that they name: `sector_sizes`: each a multiple of 128, of 1 to 5 tiles, all together 4096. `joining_table`: for every site step and site state a permutation of the 16 sectors that moves no sector by more than one place.
All inputs are finite; a program needn't handle non-finite values.
Results may differ from a plain program's by a relative error of at most 0.0065.
Values may be sent and summed in bfloat16 or wider, within the bound.
No kernel may reach another device: no remote copies, remote signals or barrier semaphores. Data moves between devices by JAX's collectives and lax.ppermute only.
A program may use at most 128 MiB of HBM per device.

v0:
```python
import jax
import jax.numpy as jnp
from jax import lax
from jax.sharding import PartitionSpec as P

TILE = 128
NSEC = 16
MAXK = 5
CHANS = 8
SPAN = 2 * MAXK - 1
BF16 = jnp.bfloat16
F32 = jnp.float32


def shifted(value, steps):
    count = lax.axis_size("sector")
    pairs = [(i, i - steps) for i in range(count) if 0 <= i - steps < count]
    return lax.ppermute(value, "sector", pairs)


def pick(table, position):
    ids = jnp.arange(table.shape[-1], dtype=jnp.int32)
    return jnp.sum(jnp.where(ids == position, table, 0), axis=-1)


def layout_tables(sector_sizes, joining_table, tiles):
    counts = sector_sizes // TILE
    ids = jnp.arange(NSEC, dtype=jnp.int32)
    starts = jnp.sum(jnp.where(ids[None, :] < ids[:, None], counts[None, :], 0), axis=1)
    tile = jnp.arange(tiles, dtype=jnp.int32)
    member = (tile[:, None] >= starts[None, :]) & (tile[:, None] < (starts + counts)[None, :])

    def by_tile(per_sector):
        return jnp.sum(jnp.where(member, per_sector[..., None, :], 0), axis=-1)

    own_start = by_tile(starts)
    own_count = by_tile(counts)
    joined = joining_table[..., None] == ids
    target_start = jnp.sum(jnp.where(joined, starts, 0), axis=-1)
    anchor_start = jnp.sum(jnp.where(joined, starts[:, None], 0), axis=-2)
    anchor_count = jnp.sum(jnp.where(joined, counts[:, None], 0), axis=-2)
    return own_start, own_count, by_tile(target_start), by_tile(anchor_start), by_tile(anchor_count)


def selection(own_start, anchor_start, anchor_count, tiles):
    slot = jnp.arange(MAXK, dtype=jnp.int32)
    tile = jnp.arange(tiles, dtype=jnp.int32)
    wanted = anchor_start[:, :, None] + slot
    valid = slot < anchor_count[:, :, None]
    source = (wanted[..., None] == tile) & valid[..., None]
    block = (tile - own_start)[:, None] == slot
    return (source[..., None] & block[None, :, None, None, :]).astype(BF16)


def exchange(blocks, chosen, tiles):
    spread = lax.all_to_all(blocks, ("sector", "chan"), 0, 0, tiled=True)
    spread = spread.reshape(tiles, CHANS, 2, MAXK, TILE)
    routed = jnp.einsum(
        "snitj,tcsja->nsica", chosen, spread, preferred_element_type=F32
    ).astype(BF16)
    routed = routed.reshape(tiles, 2 * MAXK * CHANS, TILE)
    landed = lax.all_to_all(routed, "sector", 0, 0, tiled=True)
    return landed.reshape(tiles, 2, MAXK, CHANS, TILE)


def per_device(environment, sector_sizes, joining_table, isometry, mixing):
    tiles = lax.axis_size("sector")
    position = lax.axis_index("sector")
    chan = lax.axis_index("chan")
    window = environment.shape[2]
    part = window // CHANS
    fine = TILE // CHANS

    slices = lax.dynamic_slice_in_dim(isometry, chan * part, part, 2)
    own_start, own_count, target_start, anchor_start, anchor_count = layout_tables(
        sector_sizes, joining_table, tiles
    )
    my_start = pick(own_start, position)
    my_width = pick(own_count, position) * TILE
    my_target = pick(target_start, position)
    my_anchor_width = pick(anchor_count, position) * TILE

    maps = []
    for k in range(2):
        near = [slices[k] if d == 0 else shifted(slices[k], d) for d in range(-SPAN, SPAN + 1)]
        near = jnp.stack(near)
        own = lax.dynamic_slice_in_dim(near, my_start - position + SPAN, MAXK, 0)
        outs = [
            lax.dynamic_slice_in_dim(near[:, s], my_target[k, s] - position + SPAN, MAXK, 0)
            for s in range(2)
        ]
        chosen = jnp.stack([own[:, 0], own[:, 1], outs[0], outs[1]])
        full = lax.all_gather(chosen, "chan", axis=0)
        full = full.transpose(1, 0, 3, 2, 4).reshape(4, window, window)
        maps.append((full[:2], full[2:]))
    (own0, out0), (own1, out1) = maps

    column = jnp.arange(window, dtype=jnp.int32)
    masked = jnp.where(column < my_width, environment, jnp.zeros((), BF16))

    first = jnp.einsum("sjd,awj->sdwa", out0, masked, preferred_element_type=F32).astype(BF16)
    first = first.reshape(2, MAXK, CHANS, fine, 2, TILE).transpose(3, 4, 2, 0, 1, 5)
    first = first.reshape(tiles * CHANS, 2 * MAXK, TILE)
    select0 = selection(own_start, anchor_start[0], anchor_count[0], tiles)
    landed = exchange(first, select0, tiles)
    rows = landed.transpose(1, 0, 3, 2, 4).reshape(2, tiles * CHANS, window)
    second = jnp.einsum("sra,sab->srb", rows, own0, preferred_element_type=F32)
    same = jnp.eye(fine, dtype=F32)
    scale0 = 3.0 / my_anchor_width[0].astype(F32)
    weights0 = (mixing[0] * scale0[:, None, None]).reshape(2, CHANS, 2, 2 * CHANS)
    blend0 = jnp.einsum("de,scwv->dvsewc", same, weights0).reshape(fine * 2 * CHANS, -1)
    mixed = jnp.dot(blend0, second.reshape(-1, window), precision=lax.Precision.HIGHEST)
    middle = jnp.where(column < my_width, mixed, 0.0).astype(BF16)

    third = jnp.einsum("ra,sab->srb", middle, out1, preferred_element_type=F32)
    scale1 = 3.0 / my_width.astype(F32)
    weights1 = (mixing[1] * scale1).reshape(2, 2 * CHANS, CHANS, 2)
    blend1 = jnp.einsum("je,swcv->sjvcew", same, weights1).reshape(2, tiles * CHANS, -1)
    fourth = jnp.einsum("spr,srb->psb", blend1, third, precision=lax.Precision.HIGHEST).astype(BF16)
    fourth = fourth.reshape(tiles * CHANS, 2 * MAXK, TILE)
    select1 = selection(own_start, anchor_start[1], anchor_count[1], tiles)
    landed = exchange(fourth, select1, tiles)
    landed = landed.reshape(fine, 2, 2, MAXK, CHANS, TILE)
    result = jnp.einsum(
        "jvsicb,sicjd->bvd",
        landed,
        own1.reshape(2, MAXK, CHANS, fine, window),
        preferred_element_type=F32,
    )
    return jnp.where(column < my_width, result, 0.0).astype(BF16)


def solution(mesh):
    placed = (P("sector", "chan", None), P(), P(), P(None, None, None, "sector"), P())
    return jax.shard_map(
        per_device, mesh=mesh, in_specs=placed, out_specs=P("sector", "chan", None), check_vma=False
    )
```

profile of v0, /device:TPU:32, one launch (start us, length us, event | category | flops | bytes accessed | tf_op | source)
XLA Modules:
  0.0 338.2 jit_solution(9328809477865191852)
XLA Ops:
  7.3 4.7 %collective-permute-start.18 = (bf16[2,80,128]{2,1,0:T(8,128)(2,1)S(1)}, bf16[2,80,128]{2,1,0:T(8,128)(2,1)S(1)}, u32[]{:S(2)}, u32[]{:S(2)}) collective-permute-start(bf16[2,80,128]{2,1,0:T(8,128)(2,1)S(1)} %dynamic-slice_bitcast_fusion.8), channel_id=1, source_target_pairs={{0,72},{8,80},{16,88},{24,96},{32,104},{40,112},{48,120},{56,128},... | collective-permute-start | bytes 122888 | tf_op jit(solution)/shard_map/ppermute | solution.py:18
  12.1 3.4 %collective-permute-start.19 = (bf16[2,80,128]{2,1,0:T(8,128)(2,1)S(1)}, bf16[2,80,128]{2,1,0:T(8,128)(2,1)S(1)}, u32[]{:S(2)}, u32[]{:S(2)}) collective-permute-start(bf16[2,80,128]{2,1,0:T(8,128)(2,1)S(1)} %dynamic-slice_bitcast_fusion.8), channel_id=1, source_target_pairs={{0,64},{8,72},{16,80},{24,88},{32,96},{40,104},{48,112},{56,120},{... | collective-permute-start | bytes 122888 | tf_op jit(solution)/shard_map/ppermute | solution.py:18
  15.5 2.7 collective-permute-start.20
  18.1 7.3 %collective-permute-start.21 = (bf16[2,80,128]{2,1,0:T(8,128)(2,1)S(1)}, bf16[2,80,128]{2,1,0:T(8,128)(2,1)S(1)}, u32[]{:S(2)}, u32[]{:S(2)}) collective-permute-start(bf16[2,80,128]{2,1,0:T(8,128)(2,1)S(1)} %dynamic-slice_bitcast_fusion.8), channel_id=1, source_target_pairs={{0,48},{8,56},{16,64},{24,72},{32,80},{40,88},{48,96},{56,104},{64... | collective-permute-start | bytes 122888 | tf_op jit(solution)/shard_map/ppermute | solution.py:18
  25.4 4.5 %collective-permute-start.22 = (bf16[2,80,128]{2,1,0:T(8,128)(2,1)S(1)}, bf16[2,80,128]{2,1,0:T(8,128)(2,1)S(1)}, u32[]{:S(2)}, u32[]{:S(2)}) collective-permute-start(bf16[2,80,128]{2,1,0:T(8,128)(2,1)S(1)} %dynamic-slice_bitcast_fusion.8), channel_id=1, source_target_pairs={{0,40},{8,48},{16,56},{24,64},{32,72},{40,80},{48,88},{56,96},{64,... | collective-permute-start | bytes 122888 | tf_op jit(solution)/shard_map/ppermute | solution.py:18
  35.9 3.2 collective-permute-start.23
  39.2 5.1 %collective-permute-start.24 = (bf16[2,80,128]{2,1,0:T(8,128)(2,1)S(1)}, bf16[2,80,128]{2,1,0:T(8,128)(2,1)S(1)}, u32[]{:S(2)}, u32[]{:S(2)}) collective-permute-start(bf16[2,80,128]{2,1,0:T(8,128)(2,1)S(1)} %dynamic-slice_bitcast_fusion.8), channel_id=1, source_target_pairs={{0,24},{8,32},{16,40},{24,48},{32,56},{40,64},{48,72},{56,80},{64,... | collective-permute-start | bytes 122888 | tf_op jit(solution)/shard_map/ppermute | solution.py:18
  46.5 2.9 collective-permute-start.26
  49.5 2.9 collective-permute-start.27
  61.2 2.7 collective-permute-done.29
  68.6 3.2 collective-permute-done.32
  71.9 3.1 collective-permute-done.33
  76.1 3.5 %collective-permute-done.35 = bf16[2,80,128]{2,1,0:T(8,128)(2,1)S(1)} collective-permute-done((bf16[2,80,128]{2,1,0:T(8,128)(2,1)S(1)}, bf16[2,80,128]{2,1,0:T(8,128)(2,1)S(1)}, u32[]{:S(2)}, u32[]{:S(2)}) %collective-permute-start.35) | collective-permute-done | bytes 40992 | tf_op jit(solution)/shard_map/ppermute | solution.py:18
  80.6 6.5 %collective-permute-start = (bf16[2,80,128]{2,1,0:T(8,128)(2,1)S(1)}, bf16[2,80,128]{2,1,0:T(8,128)(2,1)S(1)}, u32[]{:S(2)}, u32[]{:S(2)}) collective-permute-start(bf16[2,80,128]{2,1,0:T(8,128)(2,1)S(1)} %get-tuple-element.28), channel_id=1, source_target_pairs={{0,72},{8,80},{16,88},{24,96},{32,104},{40,112},{48,120},{56,128},... | collective-permute-start | bytes 122888 | tf_op jit(solution)/shard_map/ppermute | solution.py:18
  88.4 4.8 %collective-permute-start.1 = (bf16[2,80,128]{2,1,0:T(8,128)(2,1)S(1)}, bf16[2,80,128]{2,1,0:T(8,128)(2,1)S(1)}, u32[]{:S(2)}, u32[]{:S(2)}) collective-permute-start(bf16[2,80,128]{2,1,0:T(8,128)(2,1)S(1)} %get-tuple-element.28), channel_id=1, source_target_pairs={{0,64},{8,72},{16,80},{24,88},{32,96},{40,104},{48,112},{56,120},{... | collective-permute-start | bytes 122888 | tf_op jit(solution)/shard_map/ppermute | solution.py:18
  93.1 2.5 collective-permute-start.2
  95.7 4.5 %collective-permute-start.3 = (bf16[2,80,128]{2,1,0:T(8,128)(2,1)S(1)}, bf16[2,80,128]{2,1,0:T(8,128)(2,1)S(1)}, u32[]{:S(2)}, u32[]{:S(2)}) collective-permute-start(bf16[2,80,128]{2,1,0:T(8,128)(2,1)S(1)} %get-tuple-element.28), channel_id=1, source_target_pairs={{0,48},{8,56},{16,64},{24,72},{32,80},{40,88},{48,96},{56,104},{64... | collective-permute-start | bytes 122888 | tf_op jit(solution)/shard_map/ppermute | solution.py:18
  100.2 3.5 %collective-permute-start.4 = (bf16[2,80,128]{2,1,0:T(8,128)(2,1)S(1)}, bf16[2,80,128]{2,1,0:T(8,128)(2,1)S(1)}, u32[]{:S(2)}, u32[]{:S(2)}) collective-permute-start(bf16[2,80,128]{2,1,0:T(8,128)(2,1)S(1)} %get-tuple-element.28), channel_id=1, source_target_pairs={{0,40},{8,48},{16,56},{24,64},{32,72},{40,80},{48,88},{56,96},{64,... | collective-permute-start | bytes 122888 | tf_op jit(solution)/shard_map/ppermute | solution.py:18
  103.8 3.8 %collective-permute-start.5 = (bf16[2,80,128]{2,1,0:T(8,128)(2,1)S(1)}, bf16[2,80,128]{2,1,0:T(8,128)(2,1)S(1)}, u32[]{:S(2)}, u32[]{:S(2)}) collective-permute-start(bf16[2,80,128]{2,1,0:T(8,128)(2,1)S(1)} %get-tuple-element.28), channel_id=1, source_target_pairs={{0,32},{8,40},{16,48},{24,56},{32,64},{40,72},{48,80},{56,88},{64,... | collective-permute-start | bytes 122888 | tf_op jit(solution)/shard_map/ppermute | solution.py:18
  107.6 4.5 %collective-permute-start.6 = (bf16[2,80,128]{2,1,0:T(8,128)(2,1)S(1)}, bf16[2,80,128]{2,1,0:T(8,128)(2,1)S(1)}, u32[]{:S(2)}, u32[]{:S(2)}) collective-permute-start(bf16[2,80,128]{2,1,0:T(8,128)(2,1)S(1)} %get-tuple-element.28), channel_id=1, source_target_pairs={{0,24},{8,32},{16,40},{24,48},{32,56},{40,64},{48,72},{56,80},{64,... | collective-permute-start | bytes 122888 | tf_op jit(solution)/shard_map/ppermute | solution.py:18
  112.1 2.9 collective-permute-start.7
  115.1 3.1 collective-permute-start.8
  118.2 2.7 collective-permute-start.9
  132.9 2.2 collective-permute-done.12
  137.3 3.1 collective-permute-done.14
  140.4 2.2 collective-permute-done.15
  144.5 3.7 %collective-permute-done.17 = bf16[2,80,128]{2,1,0:T(8,128)(2,1)S(1)} collective-permute-done((bf16[2,80,128]{2,1,0:T(8,128)(2,1)S(1)}, bf16[2,80,128]{2,1,0:T(8,128)(2,1)S(1)}, u32[]{:S(2)}, u32[]{:S(2)}) %collective-permute-start.17) | collective-permute-done | bytes 40992 | tf_op jit(solution)/shard_map/ppermute | solution.py:18
  150.8 3.3 copy.158
  154.1 2.4 fusion.41
  156.5 4.8 %reshape.140 = bf16[2,640,640,1]{2,1,0,3:T(8,128)(2,1)} reshape(bf16[2,8,80,5,128]{4,3,2,1,0:T(8,128)(2,1)} %get-tuple-element.15) | data formatting | bytes 3276800 | tf_op jit(solution)/shard_map/slice | solution.py:95
  161.3 2.2 fusion.9
  167.4 16.6 %all-to-all-start = ((bf16[256,10,128]{2,1,0:T(8,128)(2,1)}), bf16[256,10,128]{2,1,0:T(8,128)(2,1)}, u32[]{:S(2)}, u32[]{:S(2)}) async-start(bf16[256,10,128]{2,1,0:T(8,128)(2,1)} %copy.98), calls=%async_computation | async-start | bytes 2097152 | tf_op jit(solution)/shard_map/all_to_all | solution.py:56
  184.3 29.3 %all-to-all-done = bf16[256,10,128]{2,1,0:T(8,128)(2,1)} async-done(((bf16[256,10,128]{2,1,0:T(8,128)(2,1)}), bf16[256,10,128]{2,1,0:T(8,128)(2,1)}, u32[]{:S(2)}, u32[]{:S(2)}) %all-to-all-start) | async-done | bytes 655392 | tf_op jit(solution)/shard_map/all_to_all | solution.py:56
  216.6 5.8 %all-to-all-start.1 = ((bf16[32,80,128]{2,1,0:T(8,128)(2,1)}), bf16[32,80,128]{2,1,0:T(8,128)(2,1)S(1)}, u32[]{:S(2)}, u32[]{:S(2)}) async-start(bf16[32,80,128]{2,1,0:T(8,128)(2,1)} %bitcast.251), calls=%async_computation.1 | async-start | bytes 1310720 | tf_op jit(solution)/shard_map/all_to_all | solution.py:62
  222.3 2.6 multiply_bitcast_fusion.1
  224.9 4.2 %reshape.125 = f32[256,512]{0,1:T(8,128)} reshape(f32[16,16,2,16,2,8]{1,0,5,4,3,2:T(8,128)} %multiply_bitcast_fusion.1) | data formatting | bytes 1048576 | tf_op jit(solution)/shard_map/reshape | solution.py:111
  229.3 2.6 multiply_bitcast_fusion
  231.8 4.2 %reshape.133 = f32[2,256,256]{2,1,0:T(8,128)} reshape(f32[2,16,2,8,16,16]{5,4,3,2,1,0:T(8,128)} %multiply_bitcast_fusion) | data formatting | bytes 1048576 | tf_op jit(solution)/shard_map/reshape | solution.py:118
  236.0 3.0 slice.145
  239.0 3.3 copy.159
  242.3 2.5 fusion.42
  244.7 4.7 %slice.130 = bf16[2,640,640]{2,1,0:T(8,128)(2,1)} reshape(bf16[2,8,80,5,128]{4,3,2,1,0:T(8,128)(2,1)} %get-tuple-element.17) | data formatting | bytes 3276800 | tf_op jit(solution)/shard_map/slice | solution.py:95
  249.4 2.2 fusion.26
  257.3 12.5 %all-to-all-start.2 = ((bf16[256,10,128]{2,1,0:T(8,128)(2,1)}), bf16[256,10,128]{2,1,0:T(8,128)(2,1)}, u32[]{:S(2)}, u32[]{:S(2)}) async-start(bf16[256,10,128]{2,1,0:T(8,128)(2,1)} %copy.107), calls=%async_computation.2 | async-start | bytes 2097152 | tf_op jit(solution)/shard_map/all_to_all | solution.py:56
  270.0 29.4 %all-to-all-done.2 = bf16[256,10,128]{2,1,0:T(8,128)(2,1)} async-done(((bf16[256,10,128]{2,1,0:T(8,128)(2,1)}), bf16[256,10,128]{2,1,0:T(8,128)(2,1)}, u32[]{:S(2)}, u32[]{:S(2)}) %all-to-all-start.2) | async-done | bytes 655392 | tf_op jit(solution)/shard_map/all_to_all | solution.py:56
  302.4 5.8 %all-to-all-start.3 = ((bf16[32,80,128]{2,1,0:T(8,128)(2,1)}), bf16[32,80,128]{2,1,0:T(8,128)(2,1)S(1)}, u32[]{:S(2)}, u32[]{:S(2)}) async-start(bf16[32,80,128]{2,1,0:T(8,128)(2,1)} %bitcast.109), calls=%async_computation.3 | async-start | bytes 1310720 | tf_op jit(solution)/shard_map/all_to_all | solution.py:62
  308.2 3.0 reshape.124
  311.2 16.9 %all-to-all-done.3 = bf16[32,80,128]{2,1,0:T(8,128)(2,1)S(1)} async-done(((bf16[32,80,128]{2,1,0:T(8,128)(2,1)}), bf16[32,80,128]{2,1,0:T(8,128)(2,1)S(1)}, u32[]{:S(2)}, u32[]{:S(2)}) %all-to-all-start.3) | async-done | bytes 655392 | tf_op jit(solution)/shard_map/all_to_all | solution.py:62
  (155 shorter events, 59.8 us)
Async XLA Ops:
  6.5 144.3 %all-gather.7.cloned.1.call-start = ((), (), s32[]{:S(2)}) async-start(), calls=%async_computation.5 | async-start | bytes 3686400 | tf_op jit(solution)/shard_map/all_gather | solution.py:93
  7.3 28.6 %collective-permute-start.18 = (bf16[2,80,128]{2,1,0:T(8,128)(2,1)S(1)}, bf16[2,80,128]{2,1,0:T(8,128)(2,1)S(1)}, u32[]{:S(2)}, u32[]{:S(2)}) collective-permute-start(bf16[2,80,128]{2,1,0:T(8,128)(2,1)S(1)} %dynamic-slice_bitcast_fusion.8), channel_id=1, source_target_pairs={{0,72},{8,80},{16,88},{24,96},{32,104},{40,112},{48,120},{56,128},... | collective-permute-start | bytes 122888 | tf_op jit(solution)/shard_map/ppermute | solution.py:18
  12.1 27.1 %collective-permute-start.19 = (bf16[2,80,128]{2,1,0:T(8,128)(2,1)S(1)}, bf16[2,80,128]{2,1,0:T(8,128)(2,1)S(1)}, u32[]{:S(2)}, u32[]{:S(2)}) collective-permute-start(bf16[2,80,128]{2,1,0:T(8,128)(2,1)S(1)} %dynamic-slice_bitcast_fusion.8), channel_id=1, source_target_pairs={{0,64},{8,72},{16,80},{24,88},{32,96},{40,104},{48,112},{56,120},{... | collective-permute-start | bytes 122888 | tf_op jit(solution)/shard_map/ppermute | solution.py:18
  15.5 28.8 %collective-permute-start.20 = (bf16[2,80,128]{2,1,0:T(8,128)(2,1)S(1)}, bf16[2,80,128]{2,1,0:T(8,128)(2,1)S(1)}, u32[]{:S(2)}, u32[]{:S(2)}) collective-permute-start(bf16[2,80,128]{2,1,0:T(8,128)(2,1)S(1)} %dynamic-slice_bitcast_fusion.8), channel_id=1, source_target_pairs={{0,56},{8,64},{16,72},{24,80},{32,88},{40,96},{48,104},{56,112},{6... | collective-permute-start | bytes 122888 | tf_op jit(solution)/shard_map/ppermute | solution.py:18
  18.1 28.4 %collective-permute-start.21 = (bf16[2,80,128]{2,1,0:T(8,128)(2,1)S(1)}, bf16[2,80,128]{2,1,0:T(8,128)(2,1)S(1)}, u32[]{:S(2)}, u32[]{:S(2)}) collective-permute-start(bf16[2,80,128]{2,1,0:T(8,128)(2,1)S(1)} %dynamic-slice_bitcast_fusion.8), channel_id=1, source_target_pairs={{0,48},{8,56},{16,64},{24,72},{32,80},{40,88},{48,96},{56,104},{64... | collective-permute-start | bytes 122888 | tf_op jit(solution)/shard_map/ppermute | solution.py:18
  25.4 24.0 %collective-permute-start.22 = (bf16[2,80,128]{2,1,0:T(8,128)(2,1)S(1)}, bf16[2,80,128]{2,1,0:T(8,128)(2,1)S(1)}, u32[]{:S(2)}, u32[]{:S(2)}) collective-permute-start(bf16[2,80,128]{2,1,0:T(8,128)(2,1)S(1)} %dynamic-slice_bitcast_fusion.8), channel_id=1, source_target_pairs={{0,40},{8,48},{16,56},{24,64},{32,72},{40,80},{48,88},{56,96},{64,... | collective-permute-start | bytes 122888 | tf_op jit(solution)/shard_map/ppermute | solution.py:18
  35.9 16.5 %collective-permute-start.23 = (bf16[2,80,128]{2,1,0:T(8,128)(2,1)S(1)}, bf16[2,80,128]{2,1,0:T(8,128)(2,1)S(1)}, u32[]{:S(2)}, u32[]{:S(2)}) collective-permute-start(bf16[2,80,128]{2,1,0:T(8,128)(2,1)S(1)} %dynamic-slice_bitcast_fusion.8), channel_id=1, source_target_pairs={{0,32},{8,40},{16,48},{24,56},{32,64},{40,72},{48,80},{56,88},{64,... | collective-permute-start | bytes 122888 | tf_op jit(solution)/shard_map/ppermute | solution.py:18
  39.2 14.6 %collective-permute-start.24 = (bf16[2,80,128]{2,1,0:T(8,128)(2,1)S(1)}, bf16[2,80,128]{2,1,0:T(8,128)(2,1)S(1)}, u32[]{:S(2)}, u32[]{:S(2)}) collective-permute-start(bf16[2,80,128]{2,1,0:T(8,128)(2,1)S(1)} %dynamic-slice_bitcast_fusion.8), channel_id=1, source_target_pairs={{0,24},{8,32},{16,40},{24,48},{32,56},{40,64},{48,72},{56,80},{64,... | collective-permute-start | bytes 122888 | tf_op jit(solution)/shard_map/ppermute | solution.py:18
  44.3 10.8 %collective-permute-start.25 = (bf16[2,80,128]{2,1,0:T(8,128)(2,1)S(1)}, bf16[2,80,128]{2,1,0:T(8,128)(2,1)S(1)}, u32[]{:S(2)}, u32[]{:S(2)}) collective-permute-start(bf16[2,80,128]{2,1,0:T(8,128)(2,1)S(1)} %dynamic-slice_bitcast_fusion.8), channel_id=1, source_target_pairs={{0,16},{8,24},{16,32},{24,40},{32,48},{40,56},{48,64},{56,72},{64,... | collective-permute-start | bytes 122888 | tf_op jit(solution)/shard_map/ppermute | solution.py:18
  46.5 9.9 %collective-permute-start.26 = (bf16[2,80,128]{2,1,0:T(8,128)(2,1)S(1)}, bf16[2,80,128]{2,1,0:T(8,128)(2,1)S(1)}, u32[]{:S(2)}, u32[]{:S(2)}) collective-permute-start(bf16[2,80,128]{2,1,0:T(8,128)(2,1)S(1)} %dynamic-slice_bitcast_fusion.8), channel_id=1, source_target_pairs={{0,8},{8,16},{16,24},{24,32},{32,40},{40,48},{48,56},{56,64},{64,7... | collective-permute-start | bytes 122888 | tf_op jit(solution)/shard_map/ppermute | solution.py:18
  49.5 9.1 %collective-permute-start.27 = (bf16[2,80,128]{2,1,0:T(8,128)(2,1)S(1)}, bf16[2,80,128]{2,1,0:T(8,128)(2,1)S(1)}, u32[]{:S(2)}, u32[]{:S(2)}) collective-permute-start(bf16[2,80,128]{2,1,0:T(8,128)(2,1)S(1)} %dynamic-slice_bitcast_fusion.8), channel_id=1, source_target_pairs={{8,0},{16,8},{24,16},{32,24},{40,32},{48,40},{56,48},{64,56},{72,6... | collective-permute-start | bytes 122888 | tf_op jit(solution)/shard_map/ppermute | solution.py:18
  52.4 7.5 %collective-permute-start.28 = (bf16[2,80,128]{2,1,0:T(8,128)(2,1)S(1)}, bf16[2,80,128]{2,1,0:T(8,128)(2,1)S(1)}, u32[]{:S(2)}, u32[]{:S(2)}) collective-permute-start(bf16[2,80,128]{2,1,0:T(8,128)(2,1)S(1)} %dynamic-slice_bitcast_fusion.8), channel_id=1, source_target_pairs={{16,0},{24,8},{32,16},{40,24},{48,32},{56,40},{64,48},{72,56},{80,... | collective-permute-start | bytes 122888 | tf_op jit(solution)/shard_map/ppermute | solution.py:18
  53.7 10.1 %collective-permute-start.29 = (bf16[2,80,128]{2,1,0:T(8,128)(2,1)S(1)}, bf16[2,80,128]{2,1,0:T(8,128)(2,1)S(1)}, u32[]{:S(2)}, u32[]{:S(2)}) collective-permute-start(bf16[2,80,128]{2,1,0:T(8,128)(2,1)S(1)} %dynamic-slice_bitcast_fusion.8), channel_id=1, source_target_pairs={{24,0},{32,8},{40,16},{48,24},{56,32},{64,40},{72,48},{80,56},{88,... | collective-permute-start | bytes 122888 | tf_op jit(solution)/shard_map/ppermute | solution.py:18
  55.1 11.4 %collective-permute-start.30 = (bf16[2,80,128]{2,1,0:T(8,128)(2,1)S(1)}, bf16[2,80,128]{2,1,0:T(8,128)(2,1)S(1)}, u32[]{:S(2)}, u32[]{:S(2)}) collective-permute-start(bf16[2,80,128]{2,1,0:T(8,128)(2,1)S(1)} %dynamic-slice_bitcast_fusion.8), channel_id=1, source_target_pairs={{32,0},{40,8},{48,16},{56,24},{64,32},{72,40},{80,48},{88,56},{96,... | collective-permute-start | bytes 122888 | tf_op jit(solution)/shard_map/ppermute | solution.py:18
  56.4 12.2 %collective-permute-start.31 = (bf16[2,80,128]{2,1,0:T(8,128)(2,1)S(1)}, bf16[2,80,128]{2,1,0:T(8,128)(2,1)S(1)}, u32[]{:S(2)}, u32[]{:S(2)}) collective-permute-start(bf16[2,80,128]{2,1,0:T(8,128)(2,1)S(1)} %dynamic-slice_bitcast_fusion.8), channel_id=1, source_target_pairs={{40,0},{48,8},{56,16},{64,24},{72,32},{80,40},{88,48},{96,56},{104... | collective-permute-start | bytes 122888 | tf_op jit(solution)/shard_map/ppermute | solution.py:18
  58.5 13.3 %collective-permute-start.32 = (bf16[2,80,128]{2,1,0:T(8,128)(2,1)S(1)}, bf16[2,80,128]{2,1,0:T(8,128)(2,1)S(1)}, u32[]{:S(2)}, u32[]{:S(2)}) collective-permute-start(bf16[2,80,128]{2,1,0:T(8,128)(2,1)S(1)} %dynamic-slice_bitcast_fusion.8), channel_id=1, source_target_pairs={{48,0},{56,8},{64,16},{72,24},{80,32},{88,40},{96,48},{104,56},{11... | collective-permute-start | bytes 122888 | tf_op jit(solution)/shard_map/ppermute | solution.py:18
  59.9 15.1 %collective-permute-start.33 = (bf16[2,80,128]{2,1,0:T(8,128)(2,1)S(1)}, bf16[2,80,128]{2,1,0:T(8,128)(2,1)S(1)}, u32[]{:S(2)}, u32[]{:S(2)}) collective-permute-start(bf16[2,80,128]{2,1,0:T(8,128)(2,1)S(1)} %dynamic-slice_bitcast_fusion.8), channel_id=1, source_target_pairs={{56,0},{64,8},{72,16},{80,24},{88,32},{96,40},{104,48},{112,56},{1... | collective-permute-start | bytes 122888 | tf_op jit(solution)/shard_map/ppermute | solution.py:18
  63.8 12.3 %collective-permute-start.34 = (bf16[2,80,128]{2,1,0:T(8,128)(2,1)S(1)}, bf16[2,80,128]{2,1,0:T(8,128)(2,1)S(1)}, u32[]{:S(2)}, u32[]{:S(2)}) collective-permute-start(bf16[2,80,128]{2,1,0:T(8,128)(2,1)S(1)} %dynamic-slice_bitcast_fusion.8), channel_id=1, source_target_pairs={{64,0},{72,8},{80,16},{88,24},{96,32},{104,40},{112,48},{120,56},{... | collective-permute-start | bytes 122888 | tf_op jit(solution)/shard_map/ppermute | solution.py:18
  66.5 13.1 %collective-permute-start.35 = (bf16[2,80,128]{2,1,0:T(8,128)(2,1)S(1)}, bf16[2,80,128]{2,1,0:T(8,128)(2,1)S(1)}, u32[]{:S(2)}, u32[]{:S(2)}) collective-permute-start(bf16[2,80,128]{2,1,0:T(8,128)(2,1)S(1)} %dynamic-slice_bitcast_fusion.8), channel_id=1, source_target_pairs={{72,0},{80,8},{88,16},{96,24},{104,32},{112,40},{120,48},{128,56},... | collective-permute-start | bytes 122888 | tf_op jit(solution)/shard_map/ppermute | solution.py:18
  80.6 158.4 %all-gather.5.cloned.1.call-start = ((), (), s32[]{:S(2)}) async-start(), calls=%async_computation.4 | async-start | bytes 3686400 | tf_op jit(solution)/shard_map/all_gather | solution.py:93
  80.6 23.1 %collective-permute-start = (bf16[2,80,128]{2,1,0:T(8,128)(2,1)S(1)}, bf16[2,80,128]{2,1,0:T(8,128)(2,1)S(1)}, u32[]{:S(2)}, u32[]{:S(2)}) collective-permute-start(bf16[2,80,128]{2,1,0:T(8,128)(2,1)S(1)} %get-tuple-element.28), channel_id=1, source_target_pairs={{0,72},{8,80},{16,88},{24,96},{32,104},{40,112},{48,120},{56,128},... | collective-permute-start | bytes 122888 | tf_op jit(solution)/shard_map/ppermute | solution.py:18
  88.4 19.3 %collective-permute-start.1 = (bf16[2,80,128]{2,1,0:T(8,128)(2,1)S(1)}, bf16[2,80,128]{2,1,0:T(8,128)(2,1)S(1)}, u32[]{:S(2)}, u32[]{:S(2)}) collective-permute-start(bf16[2,80,128]{2,1,0:T(8,128)(2,1)S(1)} %get-tuple-element.28), channel_id=1, source_target_pairs={{0,64},{8,72},{16,80},{24,88},{32,96},{40,104},{48,112},{56,120},{... | collective-permute-start | bytes 122888 | tf_op jit(solution)/shard_map/ppermute | solution.py:18
  93.1 19.0 %collective-permute-start.2 = (bf16[2,80,128]{2,1,0:T(8,128)(2,1)S(1)}, bf16[2,80,128]{2,1,0:T(8,128)(2,1)S(1)}, u32[]{:S(2)}, u32[]{:S(2)}) collective-permute-start(bf16[2,80,128]{2,1,0:T(8,128)(2,1)S(1)} %get-tuple-element.28), channel_id=1, source_target_pairs={{0,56},{8,64},{16,72},{24,80},{32,88},{40,96},{48,104},{56,112},{6... | collective-permute-start | bytes 122888 | tf_op jit(solution)/shard_map/ppermute | solution.py:18
  95.7 19.4 %collective-permute-start.3 = (bf16[2,80,128]{2,1,0:T(8,128)(2,1)S(1)}, bf16[2,80,128]{2,1,0:T(8,128)(2,1)S(1)}, u32[]{:S(2)}, u32[]{:S(2)}) collective-permute-start(bf16[2,80,128]{2,1,0:T(8,128)(2,1)S(1)} %get-tuple-element.28), channel_id=1, source_target_pairs={{0,48},{8,56},{16,64},{24,72},{32,80},{40,88},{48,96},{56,104},{64... | collective-permute-start | bytes 122888 | tf_op jit(solution)/shard_map/ppermute | solution.py:18
  100.2 18.0 %collective-permute-start.4 = (bf16[2,80,128]{2,1,0:T(8,128)(2,1)S(1)}, bf16[2,80,128]{2,1,0:T(8,128)(2,1)S(1)}, u32[]{:S(2)}, u32[]{:S(2)}) collective-permute-start(bf16[2,80,128]{2,1,0:T(8,128)(2,1)S(1)} %get-tuple-element.28), channel_id=1, source_target_pairs={{0,40},{8,48},{16,56},{24,64},{32,72},{40,80},{48,88},{56,96},{64,... | collective-permute-start | bytes 122888 | tf_op jit(solution)/shard_map/ppermute | solution.py:18
  103.8 17.2 %collective-permute-start.5 = (bf16[2,80,128]{2,1,0:T(8,128)(2,1)S(1)}, bf16[2,80,128]{2,1,0:T(8,128)(2,1)S(1)}, u32[]{:S(2)}, u32[]{:S(2)}) collective-permute-start(bf16[2,80,128]{2,1,0:T(8,128)(2,1)S(1)} %get-tuple-element.28), channel_id=1, source_target_pairs={{0,32},{8,40},{16,48},{24,56},{32,64},{40,72},{48,80},{56,88},{64,... | collective-permute-start | bytes 122888 | tf_op jit(solution)/shard_map/ppermute | solution.py:18
  107.6 14.7 %collective-permute-start.6 = (bf16[2,80,128]{2,1,0:T(8,128)(2,1)S(1)}, bf16[2,80,128]{2,1,0:T(8,128)(2,1)S(1)}, u32[]{:S(2)}, u32[]{:S(2)}) collective-permute-start(bf16[2,80,128]{2,1,0:T(8,128)(2,1)S(1)} %get-tuple-element.28), channel_id=1, source_target_pairs={{0,24},{8,32},{16,40},{24,48},{32,56},{40,64},{48,72},{56,80},{64,... | collective-permute-start | bytes 122888 | tf_op jit(solution)/shard_map/ppermute | solution.py:18
  112.1 11.5 %collective-permute-start.7 = (bf16[2,80,128]{2,1,0:T(8,128)(2,1)S(1)}, bf16[2,80,128]{2,1,0:T(8,128)(2,1)S(1)}, u32[]{:S(2)}, u32[]{:S(2)}) collective-permute-start(bf16[2,80,128]{2,1,0:T(8,128)(2,1)S(1)} %get-tuple-element.28), channel_id=1, source_target_pairs={{0,16},{8,24},{16,32},{24,40},{32,48},{40,56},{48,64},{56,72},{64,... | collective-permute-start | bytes 122888 | tf_op jit(solution)/shard_map/ppermute | solution.py:18
  115.1 9.9 %collective-permute-start.8 = (bf16[2,80,128]{2,1,0:T(8,128)(2,1)S(1)}, bf16[2,80,128]{2,1,0:T(8,128)(2,1)S(1)}, u32[]{:S(2)}, u32[]{:S(2)}) collective-permute-start(bf16[2,80,128]{2,1,0:T(8,128)(2,1)S(1)} %get-tuple-element.28), channel_id=1, source_target_pairs={{0,8},{8,16},{16,24},{24,32},{32,40},{40,48},{48,56},{56,64},{64,7... | collective-permute-start | bytes 122888 | tf_op jit(solution)/shard_map/ppermute | solution.py:18
  118.2 8.9 %collective-permute-start.9 = (bf16[2,80,128]{2,1,0:T(8,128)(2,1)S(1)}, bf16[2,80,128]{2,1,0:T(8,128)(2,1)S(1)}, u32[]{:S(2)}, u32[]{:S(2)}) collective-permute-start(bf16[2,80,128]{2,1,0:T(8,128)(2,1)S(1)} %get-tuple-element.28), channel_id=1, source_target_pairs={{8,0},{16,8},{24,16},{32,24},{40,32},{48,40},{56,48},{64,56},{72,6... | collective-permute-start | bytes 122888 | tf_op jit(solution)/shard_map/ppermute | solution.py:18
  121.0 7.4 %collective-permute-start.10 = (bf16[2,80,128]{2,1,0:T(8,128)(2,1)S(1)}, bf16[2,80,128]{2,1,0:T(8,128)(2,1)S(1)}, u32[]{:S(2)}, u32[]{:S(2)}) collective-permute-start(bf16[2,80,128]{2,1,0:T(8,128)(2,1)S(1)} %get-tuple-element.28), channel_id=1, source_target_pairs={{16,0},{24,8},{32,16},{40,24},{48,32},{56,40},{64,48},{72,56},{80,... | collective-permute-start | bytes 122888 | tf_op jit(solution)/shard_map/ppermute | solution.py:18
  122.3 9.3 %collective-permute-start.11 = (bf16[2,80,128]{2,1,0:T(8,128)(2,1)S(1)}, bf16[2,80,128]{2,1,0:T(8,128)(2,1)S(1)}, u32[]{:S(2)}, u32[]{:S(2)}) collective-permute-start(bf16[2,80,128]{2,1,0:T(8,128)(2,1)S(1)} %get-tuple-element.28), channel_id=1, source_target_pairs={{24,0},{32,8},{40,16},{48,24},{56,32},{64,40},{72,48},{80,56},{88,... | collective-permute-start | bytes 122888 | tf_op jit(solution)/shard_map/ppermute | solution.py:18
  123.7 11.4 %collective-permute-start.12 = (bf16[2,80,128]{2,1,0:T(8,128)(2,1)S(1)}, bf16[2,80,128]{2,1,0:T(8,128)(2,1)S(1)}, u32[]{:S(2)}, u32[]{:S(2)}) collective-permute-start(bf16[2,80,128]{2,1,0:T(8,128)(2,1)S(1)} %get-tuple-element.28), channel_id=1, source_target_pairs={{32,0},{40,8},{48,16},{56,24},{64,32},{72,40},{80,48},{88,56},{96,... | collective-permute-start | bytes 122888 | tf_op jit(solution)/shard_map/ppermute | solution.py:18
  125.0 12.3 %collective-permute-start.13 = (bf16[2,80,128]{2,1,0:T(8,128)(2,1)S(1)}, bf16[2,80,128]{2,1,0:T(8,128)(2,1)S(1)}, u32[]{:S(2)}, u32[]{:S(2)}) collective-permute-start(bf16[2,80,128]{2,1,0:T(8,128)(2,1)S(1)} %get-tuple-element.28), channel_id=1, source_target_pairs={{40,0},{48,8},{56,16},{64,24},{72,32},{80,40},{88,48},{96,56},{104... | collective-permute-start | bytes 122888 | tf_op jit(solution)/shard_map/ppermute | solution.py:18
  127.1 13.3 %collective-permute-start.14 = (bf16[2,80,128]{2,1,0:T(8,128)(2,1)S(1)}, bf16[2,80,128]{2,1,0:T(8,128)(2,1)S(1)}, u32[]{:S(2)}, u32[]{:S(2)}) collective-permute-start(bf16[2,80,128]{2,1,0:T(8,128)(2,1)S(1)} %get-tuple-element.28), channel_id=1, source_target_pairs={{48,0},{56,8},{64,16},{72,24},{80,32},{88,40},{96,48},{104,56},{11... | collective-permute-start | bytes 122888 | tf_op jit(solution)/shard_map/ppermute | solution.py:18
  128.4 14.2 %collective-permute-start.15 = (bf16[2,80,128]{2,1,0:T(8,128)(2,1)S(1)}, bf16[2,80,128]{2,1,0:T(8,128)(2,1)S(1)}, u32[]{:S(2)}, u32[]{:S(2)}) collective-permute-start(bf16[2,80,128]{2,1,0:T(8,128)(2,1)S(1)} %get-tuple-element.28), channel_id=1, source_target_pairs={{56,0},{64,8},{72,16},{80,24},{88,32},{96,40},{104,48},{112,56},{1... | collective-permute-start | bytes 122888 | tf_op jit(solution)/shard_map/ppermute | solution.py:18
  131.6 12.9 %collective-permute-start.16 = (bf16[2,80,128]{2,1,0:T(8,128)(2,1)S(1)}, bf16[2,80,128]{2,1,0:T(8,128)(2,1)S(1)}, u32[]{:S(2)}, u32[]{:S(2)}) collective-permute-start(bf16[2,80,128]{2,1,0:T(8,128)(2,1)S(1)} %get-tuple-element.28), channel_id=1, source_target_pairs={{64,0},{72,8},{80,16},{88,24},{96,32},{104,40},{112,48},{120,56},{... | collective-permute-start | bytes 122888 | tf_op jit(solution)/shard_map/ppermute | solution.py:18
  135.1 13.1 %collective-permute-start.17 = (bf16[2,80,128]{2,1,0:T(8,128)(2,1)S(1)}, bf16[2,80,128]{2,1,0:T(8,128)(2,1)S(1)}, u32[]{:S(2)}, u32[]{:S(2)}) collective-permute-start(bf16[2,80,128]{2,1,0:T(8,128)(2,1)S(1)} %get-tuple-element.28), channel_id=1, source_target_pairs={{72,0},{80,8},{88,16},{96,24},{104,32},{112,40},{120,48},{128,56},... | collective-permute-start | bytes 122888 | tf_op jit(solution)/shard_map/ppermute | solution.py:18
  148.2 1.6 copy-start.4
  148.2 1.6 copy-start.3
  167.4 46.2 %all-to-all-start = ((bf16[256,10,128]{2,1,0:T(8,128)(2,1)}), bf16[256,10,128]{2,1,0:T(8,128)(2,1)}, u32[]{:S(2)}, u32[]{:S(2)}) async-start(bf16[256,10,128]{2,1,0:T(8,128)(2,1)} %copy.98), calls=%async_computation | async-start | bytes 2097152 | tf_op jit(solution)/shard_map/all_to_all | solution.py:56
  216.6 32.9 %all-to-all-start.1 = ((bf16[32,80,128]{2,1,0:T(8,128)(2,1)}), bf16[32,80,128]{2,1,0:T(8,128)(2,1)S(1)}, u32[]{:S(2)}, u32[]{:S(2)}) async-start(bf16[32,80,128]{2,1,0:T(8,128)(2,1)} %bitcast.251), calls=%async_computation.1 | async-start | bytes 1310720 | tf_op jit(solution)/shard_map/all_to_all | solution.py:62
  249.4 2.3 copy-start.2
  251.7 1.5 copy-start
  253.2 1.0 copy-start.1
  257.3 42.1 %all-to-all-start.2 = ((bf16[256,10,128]{2,1,0:T(8,128)(2,1)}), bf16[256,10,128]{2,1,0:T(8,128)(2,1)}, u32[]{:S(2)}, u32[]{:S(2)}) async-start(bf16[256,10,128]{2,1,0:T(8,128)(2,1)} %copy.107), calls=%async_computation.2 | async-start | bytes 2097152 | tf_op jit(solution)/shard_map/all_to_all | solution.py:56
  302.4 25.6 %all-to-all-start.3 = ((bf16[32,80,128]{2,1,0:T(8,128)(2,1)}), bf16[32,80,128]{2,1,0:T(8,128)(2,1)S(1)}, u32[]{:S(2)}, u32[]{:S(2)}) async-start(bf16[32,80,128]{2,1,0:T(8,128)(2,1)} %bitcast.109), calls=%async_computation.3 | async-start | bytes 1310720 | tf_op jit(solution)/shard_map/all_to_all | solution.py:62
Sparse Core Ops, SparseCore 0:
  80.7 34.6 all-gather.6
  149.3 34.5 all-gather.4
where the time goes:
time: 340 us; the launch traced here: 338 us
  starting transfers between devices  139 us (41%)
  waiting for transfers between devices  107 us (31%)
  local copies, waits for them, and re-layouts  51.2 us (15%)
  between operations  18.1 us (5%)
  other arithmetic  11.6 us (3%)
  matrix products  11 us (3%)
    ppermute x36, starting transfers between devices, shifted(): return lax.ppermute(value, 'sector', pairs)  98.4 us
    all_to_all x2, waiting for transfers between devices, exchange(): spread = lax.all_to_all(blocks, ('sector', 'chan'), 0, 0, tiled=True)  58.7 us
    ppermute x36, waiting for transfers between devices, shifted(): return lax.ppermute(value, 'sector', pairs)  31.6 us
    all_to_all x2, starting transfers between devices, exchange(): spread = lax.all_to_all(blocks, ('sector', 'chan'), 0, 0, tiled=True)  29.1 us
    slice x5, local copies, waits for them, and re-layouts, per_device(): maps.append((full[:2], full[2:]))  17.3 us
    all_to_all x2, waiting for transfers between devices, exchange(): landed = lax.all_to_all(routed, 'sector', 0, 0, tiled=True)  16.9 us
    all_to_all x2, starting transfers between devices, exchange(): landed = lax.all_to_all(routed, 'sector', 0, 0, tiled=True)  11.5 us
  transfers between devices with their start and end apart: 42, of which 17 were waited for; matrix products, arithmetic and copies ran while one was open for 17% of the time, Pallas kernels for 0%

commit v1 on v0

v1 whole, which is shorter than its diff:
```python
import jax
import jax.numpy as jnp
from jax import lax
from jax.sharding import PartitionSpec as P

TILE = 128
NSEC = 16
MAXK = 5
CHANS = 8
BF16 = jnp.bfloat16
F32 = jnp.float32


def pick(table, position):
    ids = jnp.arange(table.shape[-1], dtype=jnp.int32)
    return jnp.sum(jnp.where(ids == position, table, 0), axis=-1)


def layout_tables(sector_sizes, joining_table, tiles):
    counts = sector_sizes // TILE
    ids = jnp.arange(NSEC, dtype=jnp.int32)
    starts = jnp.sum(jnp.where(ids[None, :] < ids[:, None], counts[None, :], 0), axis=1)
    tile = jnp.arange(tiles, dtype=jnp.int32)
    member = (tile[:, None] >= starts[None, :]) & (tile[:, None] < (starts + counts)[None, :])
    joined = joining_table[..., None] == ids

    def by_tile(per_sector):
        return jnp.sum(jnp.where(member, per_sector[..., None, :], 0), axis=-1)

    def both(select):
        return by_tile(select(starts)), by_tile(select(counts))

    own = both(lambda v: v)
    target = both(lambda v: jnp.sum(jnp.where(joined, v, 0), axis=-1))
    anchor = both(lambda v: jnp.sum(jnp.where(joined, v[:, None], 0), axis=-2))
    return own, target, anchor


def sources(start, count, tiles):
    slot = jnp.arange(MAXK, dtype=jnp.int32)
    tile = jnp.arange(tiles, dtype=jnp.int32)
    wanted = jnp.where(slot < count[..., None], start[..., None] + slot, -1)
    return wanted[..., None] == tile


def selection(own_start, anchor, tiles):
    slot = jnp.arange(MAXK, dtype=jnp.int32)
    tile = jnp.arange(tiles, dtype=jnp.int32)
    block = (tile - own_start)[:, None] == slot
    return (sources(*anchor, tiles)[..., None] & block[None, :, None, None, :]).astype(BF16)


def route(chosen, spread):
    return jnp.einsum("snitj,tsjca->nsica", chosen, spread, preferred_element_type=F32).astype(BF16)


def deliver(blocks):
    return lax.all_to_all(blocks, "sector", 0, 0, tiled=True)


def per_device(environment, sector_sizes, joining_table, isometry, mixing):
    tiles = lax.axis_size("sector")
    position = lax.axis_index("sector")
    chan = lax.axis_index("chan")
    window = environment.shape[2]
    part = window // CHANS
    fine = TILE // CHANS
    piece = -(-part // tiles)

    own, target, anchor = layout_tables(sector_sizes, joining_table, tiles)
    width = pick(own[1], position) * TILE

    column = jnp.arange(window, dtype=jnp.int32)
    masked = jnp.where(column < width, environment, jnp.zeros((), BF16)).transpose(1, 0, 2)
    gathered = lax.all_gather(masked, "chan", axis=0, tiled=True)

    slim = lax.dynamic_slice_in_dim(isometry[0], chan * fine, fine, 2)
    slim = slim.transpose(0, 2, 1).reshape(2, part, TILE)
    slices = lax.dynamic_slice_in_dim(isometry, chan * part, part, 2)
    kinds = jnp.concatenate([slim[None], slices])
    kinds = jnp.pad(kinds, ((0, 0), (0, 0), (0, tiles * piece - part), (0, 0)))
    kinds = kinds.reshape(6, tiles, piece, TILE).transpose(1, 0, 2, 3)
    spread = deliver(kinds.reshape(tiles, 6 * piece, TILE)).reshape(tiles, 3, 2, piece, TILE)
    mine = jnp.broadcast_to(sources(*own, tiles), (2, tiles, MAXK, tiles)).astype(BF16)
    theirs = sources(*target, tiles).astype(BF16)
    picks = [(theirs[0], 0), (mine, 1), (theirs[1], 2), (mine, 2)]
    routed = [
        jnp.einsum("snit,tsrd->nsird", hot, spread[:, kind], preferred_element_type=F32)
        for hot, kind in picks
    ]
    routed = jnp.stack(routed, axis=1).astype(BF16)
    landed = deliver(routed.reshape(tiles, 8 * MAXK * piece, TILE))
    landed = landed.reshape(tiles, 4, 2 * MAXK, piece, TILE)

    def rows_of(groups):
        moved = groups.transpose(0, 3, 1, 2, 4)
        return moved.reshape(tiles * piece, -1)[:part]

    maps_a = lax.all_gather(rows_of(landed[:, 1:3]), "chan", axis=0, tiled=True)
    maps_b = lax.all_gather(rows_of(landed[:, 3:4]), "chan", axis=0, tiled=True)
    maps_a = maps_a.reshape(window, 2, 2, window)
    own0, out1 = maps_a[:, 0], maps_a[:, 1]
    slim = landed[:, 0].transpose(1, 0, 2, 3).reshape(2 * MAXK, tiles * piece, TILE)[:, :part]
    slim = slim.reshape(2 * MAXK * fine, window)

    first = jnp.einsum("dj,waj->wda", slim, gathered, preferred_element_type=F32).astype(BF16)
    first = first.reshape(2, CHANS, 2 * MAXK, fine, TILE).transpose(3, 0, 2, 1, 4)
    first = deliver(first.reshape(tiles, 2 * MAXK * CHANS, TILE))
    select0 = selection(own[0], (anchor[0][0], anchor[1][0]), tiles)
    first = route(select0, first.reshape(tiles, 2, MAXK, CHANS, TILE))
    first = deliver(first.reshape(tiles, 2 * MAXK * CHANS, TILE))
    rows = first.reshape(tiles, 2, MAXK, CHANS, TILE).transpose(1, 0, 3, 2, 4)
    rows = rows.reshape(2, tiles * CHANS, window)
    second = jnp.einsum("sra,asb->srb", rows, own0, preferred_element_type=F32)
    same = jnp.eye(fine, dtype=F32)
    scale0 = 3.0 / (pick(anchor[1][0], position) * TILE).astype(F32)
    weights0 = mixing[0] * scale0[:, None, None]
    blend0 = jnp.einsum("de,swv->dvsew", same, weights0).reshape(fine * 2 * CHANS, -1)
    mixed = jnp.dot(blend0, second.reshape(-1, window), precision=lax.Precision.HIGHEST)
    middle = mixed.astype(BF16)

    third = jnp.einsum("ra,asb->srb", middle, out1, preferred_element_type=F32)
    scale1 = 3.0 / width.astype(F32)
    weights1 = (mixing[1] * scale1).reshape(2, 2 * CHANS, CHANS, 2)
    blend1 = jnp.einsum("je,swcv->sjvcew", same, weights1).reshape(2, tiles * CHANS, -1)
    fourth = jnp.einsum("spr,srb->psb", blend1, third, precision=lax.Precision.HIGHEST).astype(BF16)
    fourth = fourth.reshape(tiles * CHANS, 2 * MAXK, TILE)
    fourth = lax.all_to_all(fourth, ("sector", "chan"), 0, 0, tiled=True)
    fourth = fourth.reshape(tiles, CHANS, 2, MAXK, TILE).transpose(0, 2, 3, 1, 4)
    select1 = selection(own[0], (anchor[0][1], anchor[1][1]), tiles)
    fourth = deliver(route(select1, fourth).reshape(tiles, 2 * MAXK * CHANS, TILE))
    result = jnp.einsum(
        "jvsicb,icjsd->bvd",
        fourth.reshape(fine, 2, 2, MAXK, CHANS, TILE),
        maps_b.reshape(MAXK, CHANS, fine, 2, window),
        preferred_element_type=F32,
    )
    return result.astype(BF16)


def solution(mesh):
    placed = (P("sector", "chan", None), P(), P(), P(None, None, None, "sector"), P())
    return jax.shard_map(
        per_device, mesh=mesh, in_specs=placed, out_specs=P("sector", "chan", None), check_vma=False
    )
```

time: 340 us -> 213 us (0.63)
  starting transfers between devices: 139 us -> 40.4 us
  blocking collectives: 0 us -> 30.8 us
  waiting for transfers between devices: 107 us -> 76.4 us
  local copies, waits for them, and re-layouts: 51.2 us -> 28.7 us
  between operations: 18.1 us -> 14.3 us
    ppermute x36 -> x0, starting transfers between devices: 98.4 us -> none  [shifted(): return lax.ppermute(value, 'sector', pairs)]
    ppermute x36 -> x0, waiting for transfers between devices: 31.6 us -> none  [shifted(): return lax.ppermute(value, 'sector', pairs)]
    all_to_all x0 -> x1, blocking collectives: none -> 30.8 us  [deliver(): return lax.all_to_all(blocks, 'sector', 0, 0, tiled=True)]
    slice x8 -> x5, local copies, waits for them, and re-layouts: 18.1 us -> 1.51 us  [the longest x2 1.49 us: rows_of(): return moved.reshape(tiles * piece, -1)[:part]]
    reshape x3 -> x8, local copies, waits for them, and re-layouts: 8.67 us -> 11.2 us  [the longest x1 5.12 us: per_device(): jnp.einsum('de,swv->dvsew', same, weights0).reshape(fine * 2 * CHANS, -1)]
    all_to_all x4 -> x5, waiting for transfers between devices: 75.5 us -> 76.3 us  [the longest x4 46 us: deliver(): return lax.all_to_all(blocks, 'sector', 0, 0, tiled=True)]
    all_to_all x4 -> x5, starting transfers between devices: 40.6 us -> 40.1 us  [the longest x4 27.1 us: deliver(): return lax.all_to_all(blocks, 'sector', 0, 0, tiled=True)]
    dot_general x6 -> x10, matrix products: 8.24 us -> 8.04 us  [the longest x1 2.77 us: per_device(): jnp.einsum('dj,waj->wda', slim, gathered, preferred_element_type=F32)]
  transfers between devices with their start and end apart: 42 -> 8, of which waited for: 17 -> 4; matrix products, arithmetic and copies ran while one was open for 17% -> 21% of each run, Pallas kernels for 0% -> 0%
where the time goes in v1:
time: 213 us; the launch traced here: 212 us
  waiting for transfers between devices  76.4 us (36%)
  starting transfers between devices  40.4 us (19%)
  blocking collectives  30.8 us (14%)
  local copies, waits for them, and re-layouts  28.7 us (13%)
  between operations  14.3 us (7%)
  matrix products  10.8 us (5%)
  other arithmetic  10.4 us (5%)
    all_to_all x4, waiting for transfers between devices, deliver(): return lax.all_to_all(blocks, 'sector', 0, 0, tiled=True)  46 us
    all_to_all x1, blocking collectives, deliver(): return lax.all_to_all(blocks, 'sector', 0, 0, tiled=True)  30.8 us
    all_to_all x1, waiting for transfers between devices, per_device(): fourth = lax.all_to_all(fourth, ('sector', 'chan'), 0, 0, tiled=True)  30.4 us
    all_to_all x4, starting transfers between devices, deliver(): return lax.all_to_all(blocks, 'sector', 0, 0, tiled=True)  27.1 us
    all_to_all x1, starting transfers between devices, per_device(): fourth = lax.all_to_all(fourth, ('sector', 'chan'), 0, 0, tiled=True)  13 us
    reshape x1, local copies, waits for them, and re-layouts, per_device(): jnp.einsum('de,swv->dvsew', same, weights0).reshape(fine * 2 * CHANS, -1)  5.12 us
  transfers between devices with their start and end apart: 8, of which 4 were waited for; matrix products, arithmetic and copies ran while one was open for 21% of the time, Pallas kernels for 0%

profile of v1, /device:TPU:32, one launch (start us, length us, event | category | flops | bytes accessed | tf_op | source)
XLA Modules:
  0.0 211.9 jit_solution(12295924653109444670)
XLA Ops:
  6.5 0.7 and_select_fusion
  7.4 0.7 fusion.51
  8.2 0.6 select_reduce_fusion.12
  9.5 1.8 fusion.37
  12.0 0.7 copy.86
  12.8 11.2 %all-to-all-start = ((bf16[32,18,128]{2,1,0:T(8,128)(2,1)}), bf16[32,18,128]{2,1,0:T(8,128)(2,1)S(1)}, u32[]{:S(2)}, u32[]{:S(2)}) async-start(bf16[32,18,128]{2,1,0:T(8,128)(2,1)} %copy.86), calls=%async_computation | async-start | bytes 393216 | tf_op jit(solution)/shard_map/all_to_all | solution.py:58
  24.0 0.3 select_reduce_fusion.1
  24.8 10.1 %all-to-all-done = bf16[32,18,128]{2,1,0:T(8,128)(2,1)S(1)} async-done(((bf16[32,18,128]{2,1,0:T(8,128)(2,1)}), bf16[32,18,128]{2,1,0:T(8,128)(2,1)S(1)}, u32[]{:S(2)}, u32[]{:S(2)}) %all-to-all-start) | async-done | bytes 147488 | tf_op jit(solution)/shard_map/all_to_all | solution.py:58
  35.0 0.2 fusion.22
  35.2 0.2 fusion.20
  35.4 0.2 fusion.21
  35.6 0.2 fusion.19
  36.0 0.4 copy.89
  36.4 30.8 %all_to_all.30 = bf16[32,120,128]{2,1,0:T(8,128)(2,1)S(1)} all-to-all(bf16[32,120,128]{2,1,0:T(8,128)(2,1)S(1)} %copy.89), channel_id=1, replica_groups=mesh['sector'=32,'chan'=8] {'sector'}, dimensions={0} | all-to-all | bytes 1966080 | tf_op jit(solution)/shard_map/all_to_all | solution.py:58
  67.4 0.2 copy.92
  67.7 0.3 reshape.196
  68.0 0.8 slice.90
  68.8 0.2 copy.96
  69.0 0.2 reshape.199
  69.4 2.8 %convolution_convert_fusion.1 = bf16[16,128,160]{1,2,0:T(8,128)(2,1)S(1)} fusion(bf16[16,128,640]{2,1,0:T(8,128)(2,1)} %all-gather.8.cloned.1.call-done, bf16[160,640,1]{1,0,2:T(8,128)(2,1)S(1)} %reshape.219), kind=kOutput, calls=%fused_computation.14 | convolution fusion | flops 419758080 | bytes 3481600 | tf_op jit(solution)/shard_map/dj,waj->wda/dot_general | solution.py:106
  72.2 1.1 copy.97
  73.3 5.1 %all-to-all-start.2 = ((bf16[32,80,128]{2,1,0:T(8,128)(2,1)}), bf16[32,80,128]{2,1,0:T(8,128)(2,1)S(1)}, u32[]{:S(2)}, u32[]{:S(2)}) async-start(bf16[32,80,128]{2,1,0:T(8,128)(2,1)} %bitcast.46), calls=%async_computation.2 | async-start | bytes 1310720 | tf_op jit(solution)/shard_map/all_to_all | solution.py:58
  78.7 19.5 %all-to-all-done.2 = bf16[32,80,128]{2,1,0:T(8,128)(2,1)S(1)} async-done(((bf16[32,80,128]{2,1,0:T(8,128)(2,1)}), bf16[32,80,128]{2,1,0:T(8,128)(2,1)S(1)}, u32[]{:S(2)}, u32[]{:S(2)}) %all-to-all-start.2) | async-done | bytes 655392 | tf_op jit(solution)/shard_map/all_to_all | solution.py:58
  98.2 0.5 fusion.8
  98.7 1.2 copy.99
  99.9 5.1 %all-to-all-start.3 = ((bf16[32,80,128]{2,1,0:T(8,128)(2,1)}), bf16[32,80,128]{2,1,0:T(8,128)(2,1)}, u32[]{:S(2)}, u32[]{:S(2)}) async-start(bf16[32,80,128]{2,1,0:T(8,128)(2,1)} %bitcast.55), calls=%async_computation.3 | async-start | bytes 1310720 | tf_op jit(solution)/shard_map/all_to_all | solution.py:58
  104.9 0.2 all-gather.4.cloned.1.call-start
  105.3 2.5 %multiply_bitcast_fusion.1 = f32[16,16,2,16,16]{4,3,2,1,0:T(8,128)} fusion(f32[16,16]{1,0:T(8,128)S(1)} %fusion.43, f32[2,16,16]{1,0,2:T(2,128)S(1)} %copy.94), kind=kLoop, calls=%fused_computation.1 | loop fusion | flops 131072 | bytes 527360 | tf_op jit(solution)/shard_map/de,swv->dvsew/transpose | solution.py:118
  107.9 5.1 %reshape.198 = f32[256,512]{1,0:T(8,128)} reshape(f32[16,16,2,16,16]{4,3,2,1,0:T(8,128)} %multiply_bitcast_fusion.1) | data formatting | bytes 1048576 | tf_op jit(solution)/shard_map/reshape | solution.py:118
  113.1 2.5 %multiply_bitcast_fusion = f32[2,16,2,8,16,16]{5,4,3,2,1,0:T(8,128)} fusion(f32[16,16]{1,0:T(8,128)S(1)} %fusion.43, f32[2,16,8,2]{1,2,3,0:T(8,128)S(1)} %copy.103), kind=kLoop, calls=%fused_computation | loop fusion | flops 131072 | bytes 527360 | tf_op jit(solution)/shard_map/je,swcv->sjvcew/transpose | solution.py:125
  115.6 4.2 %reshape.208 = f32[2,256,256]{2,1,0:T(8,128)} reshape(f32[2,16,2,8,16,16]{5,4,3,2,1,0:T(8,128)} %multiply_bitcast_fusion) | data formatting | bytes 1048576 | tf_op jit(solution)/shard_map/reshape | solution.py:125
  120.0 0.7 slice.88
  120.8 4.2 %copy.93 = bf16[640,2560]{0,1:T(8,128)(2,1)S(1)} copy(bf16[640,2560]{1,0:T(8,128)(2,1)} %all-gather.6.cloned.1.call-done) | data formatting | bytes 6553600 | tf_op jit(solution)/shard_map/all_gather | solution.py:99
  125.0 2.0 fusion
  126.9 1.5 fusion.18
  128.4 0.7 fusion.1
  129.1 0.3 copy-done
  129.5 1.3 convolution_convert_fusion
  130.8 1.7 copy.104
  132.5 13.0 %all-to-all-start.4 = ((bf16[256,10,128]{2,1,0:T(8,128)(2,1)}), bf16[256,10,128]{2,1,0:T(8,128)(2,1)S(1)}, u32[]{:S(2)}, u32[]{:S(2)}) async-start(bf16[256,10,128]{2,1,0:T(8,128)(2,1)} %copy.104), calls=%async_computation.4 | async-start | bytes 2097152 | tf_op jit(solution)/shard_map/all_to_all | solution.py:128
  145.6 30.4 %all-to-all-done.4 = bf16[256,10,128]{2,1,0:T(8,128)(2,1)S(1)} async-done(((bf16[256,10,128]{2,1,0:T(8,128)(2,1)}), bf16[256,10,128]{2,1,0:T(8,128)(2,1)S(1)}, u32[]{:S(2)}, u32[]{:S(2)}) %all-to-all-start.4) | async-done | bytes 655392 | tf_op jit(solution)/shard_map/all_to_all | solution.py:128
  176.1 0.5 fusion.7
  176.6 1.1 copy.107
  177.7 5.8 %all-to-all-start.5 = ((bf16[32,80,128]{2,1,0:T(8,128)(2,1)}), bf16[32,80,128]{2,1,0:T(8,128)(2,1)S(1)}, u32[]{:S(2)}, u32[]{:S(2)}) async-start(bf16[32,80,128]{2,1,0:T(8,128)(2,1)} %bitcast.77), calls=%async_computation.5 | async-start | bytes 1310720 | tf_op jit(solution)/shard_map/all_to_all | solution.py:58
  183.5 3.5 %reshape.195 = bf16[5,8,16,2,640]{4,3,2,1,0:T(2,128)(2,1)S(1)} reshape(bf16[640,1280]{1,0:T(8,128)(2,1)} %all-gather.4.cloned.1.call-done) | data formatting | bytes 3276800 | tf_op jit(solution)/shard_map/reshape | solution.py:135
  187.0 16.3 %all-to-all-done.5 = bf16[32,80,128]{2,1,0:T(8,128)(2,1)S(1)} async-done(((bf16[32,80,128]{2,1,0:T(8,128)(2,1)}), bf16[32,80,128]{2,1,0:T(8,128)(2,1)S(1)}, u32[]{:S(2)}, u32[]{:S(2)}) %all-to-all-start.5) | async-done | bytes 655392 | tf_op jit(solution)/shard_map/all_to_all | solution.py:58
  203.4 0.8 fusion.15
  204.2 1.2 copy.110
  (67 shorter events, 3.1 us)
Async XLA Ops:
  6.5 4.7 %slice-start = ((bf16[2,2,640,128]{3,2,1,0:T(8,128)(2,1)}), bf16[1,2,640,128]{3,2,1,0:T(8,128)(2,1)S(1)}, s32[]{:S(2)}) async-start(bf16[2,2,640,128]{3,2,1,0:T(8,128)(2,1)} %param.8), calls=%async_computation.9 | async-start | bytes 655360 | tf_op jit(solution)/shard_map/slice | solution.py:77
  6.5 5.1 %copy-start.2 = (bf16[2,2,640,128]{3,2,1,0:T(8,128)(2,1)S(1)}, bf16[2,2,640,128]{3,2,1,0:T(8,128)(2,1)}, u32[]{:S(2)}) copy-start(bf16[2,2,640,128]{3,2,1,0:T(8,128)(2,1)} %param.8) | copy-start | bytes 1966084
  6.5 62.9 %all-gather.8.cloned.1.call-start = ((), (), s32[]{:S(2)}) async-start(), calls=%async_computation.8 | async-start | bytes 2949120 | tf_op jit(solution)/shard_map/all_gather | solution.py:75
  11.3 12.7 %copy-start.4 = (s32[2,2,16]{2,1,0:T(2,128)S(1)}, s32[2,2,16]{2,1,0:T(2,128)}, u32[]{:S(2)}) copy-start(s32[2,2,16]{2,1,0:T(2,128)} %param.7) | copy-start | bytes 772
  12.8 22.2 %all-to-all-start = ((bf16[32,18,128]{2,1,0:T(8,128)(2,1)}), bf16[32,18,128]{2,1,0:T(8,128)(2,1)S(1)}, u32[]{:S(2)}, u32[]{:S(2)}) async-start(bf16[32,18,128]{2,1,0:T(8,128)(2,1)} %copy.86), calls=%async_computation | async-start | bytes 393216 | tf_op jit(solution)/shard_map/all_to_all | solution.py:58
  23.9 96.8 %all-gather.6.cloned.1.call-start = ((), (), s32[]{:S(2)}) async-start(), calls=%async_computation.7 | async-start | bytes 3686400 | tf_op jit(solution)/shard_map/all_gather | solution.py:99
  73.3 24.9 %all-to-all-start.2 = ((bf16[32,80,128]{2,1,0:T(8,128)(2,1)}), bf16[32,80,128]{2,1,0:T(8,128)(2,1)S(1)}, u32[]{:S(2)}, u32[]{:S(2)}) async-start(bf16[32,80,128]{2,1,0:T(8,128)(2,1)} %bitcast.46), calls=%async_computation.2 | async-start | bytes 1310720 | tf_op jit(solution)/shard_map/all_to_all | solution.py:58
  98.7 6.5 %copy-start.3 = (f32[2,2,16,16]{3,2,1,0:T(8,128)S(1)}, f32[2,2,16,16]{3,2,1,0:T(8,128)}, u32[]{:S(2)}) copy-start(f32[2,2,16,16]{3,2,1,0:T(8,128)} %param.9) | copy-start | bytes 12292
  99.9 25.1 %all-to-all-start.3 = ((bf16[32,80,128]{2,1,0:T(8,128)(2,1)}), bf16[32,80,128]{2,1,0:T(8,128)(2,1)}, u32[]{:S(2)}, u32[]{:S(2)}) async-start(bf16[32,80,128]{2,1,0:T(8,128)(2,1)} %bitcast.55), calls=%async_computation.3 | async-start | bytes 1310720 | tf_op jit(solution)/shard_map/all_to_all | solution.py:58
  104.9 78.6 %all-gather.4.cloned.1.call-start = ((), (), s32[]{:S(2)}) async-start(), calls=%async_computation.6 | async-start | bytes 1843200 | tf_op jit(solution)/shard_map/all_gather | solution.py:100
  107.9 5.1 %slice-start.1 = ((f32[2,2,16,16]{3,2,1,0:T(8,128)}), f32[1,2,16,16]{3,2,1,0:T(8,128)S(1)}, s32[]{:S(2)}) async-start(f32[2,2,16,16]{3,2,1,0:T(8,128)} %param.9), calls=%async_computation.10 | async-start | bytes 32768 | tf_op jit(solution)/shard_map/slice | solution.py:124
  125.0 2.0 copy-start.1
  128.4 1.0 copy-start
  132.5 43.5 %all-to-all-start.4 = ((bf16[256,10,128]{2,1,0:T(8,128)(2,1)}), bf16[256,10,128]{2,1,0:T(8,128)(2,1)S(1)}, u32[]{:S(2)}, u32[]{:S(2)}) async-start(bf16[256,10,128]{2,1,0:T(8,128)(2,1)} %copy.104), calls=%async_computation.4 | async-start | bytes 2097152 | tf_op jit(solution)/shard_map/all_to_all | solution.py:128
  177.7 25.6 %all-to-all-start.5 = ((bf16[32,80,128]{2,1,0:T(8,128)(2,1)}), bf16[32,80,128]{2,1,0:T(8,128)(2,1)S(1)}, u32[]{:S(2)}, u32[]{:S(2)}) async-start(bf16[32,80,128]{2,1,0:T(8,128)(2,1)} %bitcast.77), calls=%async_computation.5 | async-start | bytes 1310720 | tf_op jit(solution)/shard_map/all_to_all | solution.py:58
Sparse Core Ops, SparseCore 0:
  11.4 31.1 all-gather.7
  68.9 27.3 all-gather.5
  120.9 28.2 all-gather.3

commit v2 on v1

--- a/solution.py
+++ b/solution.py
@@ -65,43 +65,41 @@
     window = environment.shape[2]
     part = window // CHANS
     fine = TILE // CHANS
-    piece = -(-part // tiles)
+    half = tiles // 2
+    piece = part // half
+    exact = lax.Precision.HIGHEST
 
-    own, target, anchor = layout_tables(sector_sizes, joining_table, tiles)
-    width = pick(own[1], position) * TILE
-
-    column = jnp.arange(window, dtype=jnp.int32)
-    masked = jnp.where(column < width, environment, jnp.zeros((), BF16)).transpose(1, 0, 2)
-    gathered = lax.all_gather(masked, "chan", axis=0, tiled=True)
+    gathered = lax.all_gather(environment.transpose(1, 0, 2), "chan", axis=0, tiled=True)
 
     slim = lax.dynamic_slice_in_dim(isometry[0], chan * fine, fine, 2)
     slim = slim.transpose(0, 2, 1).reshape(2, part, TILE)
     slices = lax.dynamic_slice_in_dim(isometry, chan * part, part, 2)
     kinds = jnp.concatenate([slim[None], slices])
-    kinds = jnp.pad(kinds, ((0, 0), (0, 0), (0, tiles * piece - part), (0, 0)))
-    kinds = kinds.reshape(6, tiles, piece, TILE).transpose(1, 0, 2, 3)
-    spread = deliver(kinds.reshape(tiles, 6 * piece, TILE)).reshape(tiles, 3, 2, piece, TILE)
-    mine = jnp.broadcast_to(sources(*own, tiles), (2, tiles, MAXK, tiles)).astype(BF16)
+    kinds = kinds.reshape(3, tiles, piece, TILE).transpose(1, 0, 2, 3)
+    spread = deliver(kinds.reshape(tiles, 3 * piece, TILE)).reshape(tiles, 3, piece, TILE)
+
+    own, target, anchor = layout_tables(sector_sizes, joining_table, tiles)
+    width = pick(own[1], position) * TILE
+    mine = sources(*own, tiles).astype(BF16)
     theirs = sources(*target, tiles).astype(BF16)
+    theirs = jnp.where(position < half, theirs[:, 0], theirs[:, 1])
     picks = [(theirs[0], 0), (mine, 1), (theirs[1], 2), (mine, 2)]
     routed = [
-        jnp.einsum("snit,tsrd->nsird", hot, spread[:, kind], preferred_element_type=F32)
+        jnp.einsum("nit,trd->nird", hot, spread[:, kind], preferred_element_type=F32)
         for hot, kind in picks
     ]
     routed = jnp.stack(routed, axis=1).astype(BF16)
-    landed = deliver(routed.reshape(tiles, 8 * MAXK * piece, TILE))
-    landed = landed.reshape(tiles, 4, 2 * MAXK, piece, TILE)
+    landed = deliver(routed.reshape(tiles, 4 * MAXK * piece, TILE))
+    landed = landed.reshape(2, half, 4, MAXK, piece, TILE)
 
     def rows_of(groups):
-        moved = groups.transpose(0, 3, 1, 2, 4)
-        return moved.reshape(tiles * piece, -1)[:part]
+        return groups.transpose(1, 4, 2, 0, 3, 5).reshape(part, -1)
 
-    maps_a = lax.all_gather(rows_of(landed[:, 1:3]), "chan", axis=0, tiled=True)
-    maps_b = lax.all_gather(rows_of(landed[:, 3:4]), "chan", axis=0, tiled=True)
-    maps_a = maps_a.reshape(window, 2, 2, window)
-    own0, out1 = maps_a[:, 0], maps_a[:, 1]
-    slim = landed[:, 0].transpose(1, 0, 2, 3).reshape(2 * MAXK, tiles * piece, TILE)[:, :part]
-    slim = slim.reshape(2 * MAXK * fine, window)
+    maps_a = lax.all_gather(rows_of(landed[:, :, 1:3]), "chan", axis=0, tiled=True)
+    maps_b = lax.all_gather(rows_of(landed[:, :, 3:4]), "chan", axis=0, tiled=True)
+    slim = landed[:, :, 0].transpose(0, 2, 1, 3, 4).reshape(2 * MAXK * fine, window)
+    column = jnp.arange(window, dtype=jnp.int32)
+    slim = jnp.where(column < width, slim, jnp.zeros((), BF16))
 
     first = jnp.einsum("dj,waj->wda", slim, gathered, preferred_element_type=F32).astype(BF16)
     first = first.reshape(2, CHANS, 2 * MAXK, fine, TILE).transpose(3, 0, 2, 1, 4)
@@ -111,20 +109,36 @@
     first = deliver(first.reshape(tiles, 2 * MAXK * CHANS, TILE))
     rows = first.reshape(tiles, 2, MAXK, CHANS, TILE).transpose(1, 0, 3, 2, 4)
     rows = rows.reshape(2, tiles * CHANS, window)
-    second = jnp.einsum("sra,asb->srb", rows, own0, preferred_element_type=F32)
-    same = jnp.eye(fine, dtype=F32)
+
+    row = jnp.arange(tiles * CHANS, dtype=jnp.int32)
+    channel = jnp.arange(2 * CHANS, dtype=jnp.int32)
+    natural = ((row % (2 * CHANS))[:, None] == channel).astype(F32)
+    paired = 2 * (row % CHANS) + (row // CHANS) % 2
+    paired = (paired[:, None] == channel).astype(F32)
+    same = (row // (2 * CHANS))[:, None] == (row // (2 * CHANS))[None, :]
+
+    def blend(coefficients, out_rows):
+        spread_out = jnp.einsum("rv,wv->rw", out_rows, coefficients, precision=exact)
+        spread_out = jnp.einsum("rw,qw->rq", spread_out, natural, precision=exact)
+        return jnp.where(same, spread_out, 0.0)
+
     scale0 = 3.0 / (pick(anchor[1][0], position) * TILE).astype(F32)
-    weights0 = mixing[0] * scale0[:, None, None]
-    blend0 = jnp.einsum("de,swv->dvsew", same, weights0).reshape(fine * 2 * CHANS, -1)
-    mixed = jnp.dot(blend0, second.reshape(-1, window), precision=lax.Precision.HIGHEST)
+    scale1 = 3.0 / width.astype(F32)
+    mixed = jnp.zeros((tiles * CHANS, window), F32)
+    for s in range(2):
+        second = jnp.dot(
+            rows[s], maps_a[:, s * window : (s + 1) * window], preferred_element_type=F32
+        )
+        mixed = mixed + jnp.dot(blend(mixing[0, s] * scale0[s], natural), second, precision=exact)
     middle = mixed.astype(BF16)
 
-    third = jnp.einsum("ra,asb->srb", middle, out1, preferred_element_type=F32)
-    scale1 = 3.0 / width.astype(F32)
-    weights1 = (mixing[1] * scale1).reshape(2, 2 * CHANS, CHANS, 2)
-    blend1 = jnp.einsum("je,swcv->sjvcew", same, weights1).reshape(2, tiles * CHANS, -1)
-    fourth = jnp.einsum("spr,srb->psb", blend1, third, precision=lax.Precision.HIGHEST).astype(BF16)
-    fourth = fourth.reshape(tiles * CHANS, 2 * MAXK, TILE)
+    fourth = []
+    for s in range(2, 4):
+        third = jnp.dot(
+            middle, maps_a[:, s * window : (s + 1) * window], preferred_element_type=F32
+        )
+        fourth.append(jnp.dot(blend(mixing[1, s - 2] * scale1, paired), third, precision=exact))
+    fourth = jnp.stack(fourth, axis=1).astype(BF16)
     fourth = lax.all_to_all(fourth, ("sector", "chan"), 0, 0, tiled=True)
     fourth = fourth.reshape(tiles, CHANS, 2, MAXK, TILE).transpose(0, 2, 3, 1, 4)
     select1 = selection(own[0], (anchor[0][1], anchor[1][1]), tiles)

time: 213 us -> 193 us (0.906)
  local copies, waits for them, and re-layouts: 28.7 us -> 18.4 us
  other arithmetic: 10.4 us -> 2.37 us
  starting transfers between devices: 40.4 us -> 34.9 us
  matrix products: 10.8 us -> 15.9 us
  blocking collectives: 30.8 us -> 27.4 us
  waiting for transfers between devices: 76.4 us -> 79.4 us
    all_to_all x4, waiting for transfers between devices: 46 us -> 57.1 us  [deliver(): return lax.all_to_all(blocks, 'sector', 0, 0, tiled=True)]
    reshape x8 -> x4, local copies, waits for them, and re-layouts: 12.5 us -> 3.28 us  [the longest x2 2.14 us: rows_of(): return groups.transpose(1, 4, 2, 0, 3, 5).reshape(part, -1)]
    all_to_all x1, waiting for transfers between devices: 30.4 us -> 22.2 us  [per_device(): fourth = lax.all_to_all(fourth, ('sector', 'chan'), 0, 0, tiled=True)]
    transpose x3 -> x1, other arithmetic: 6.78 us -> 0.18 us  [per_device(): kinds = kinds.reshape(3, tiles, piece, TILE).transpose(1, 0, 2, 3)]
    all_to_all x1, starting transfers between devices: 13 us -> 8.05 us  [per_device(): fourth = lax.all_to_all(fourth, ('sector', 'chan'), 0, 0, tiled=True)]
    dot_general x8 -> x20, matrix products: 6.27 us -> 11 us  [the longest x4 2.25 us: blend(): jnp.einsum('rv,wv->rw', out_rows, coefficients, precision=exact)]
    all_gather x1 -> x0, local copies, waits for them, and re-layouts: 4.18 us -> none  [per_device(): maps_a = lax.all_gather(rows_of(landed[:, 1:3]), 'chan', axis=0, tiled=True)]
    all_to_all x1, blocking collectives: 30.8 us -> 27.4 us  [deliver(): return lax.all_to_all(blocks, 'sector', 0, 0, tiled=True)]
  transfers between devices with their start and end apart: 8 -> 8, of which waited for: 4 -> 5; matrix products, arithmetic and copies ran while one was open for 21% -> 17% of each run, Pallas kernels for 0% -> 0%
where the time goes in v2:
time: 193 us
  waiting for transfers between devices  79.4 us (41%)
  starting transfers between devices  34.9 us (18%)
  blocking collectives  27.4 us (14%)
  local copies, waits for them, and re-layouts  18.4 us (10%)
  matrix products  15.9 us (8%)
  between operations  14.3 us (7%)
  other arithmetic  2.37 us (1%)
    all_to_all x4, waiting for transfers between devices, deliver(): return lax.all_to_all(blocks, 'sector', 0, 0, tiled=True)  57.1 us
    all_to_all x1, blocking collectives, deliver(): return lax.all_to_all(blocks, 'sector', 0, 0, tiled=True)  27.4 us
    all_to_all x4, starting transfers between devices, deliver(): return lax.all_to_all(blocks, 'sector', 0, 0, tiled=True)  26.5 us
    all_to_all x1, waiting for transfers between devices, per_device(): fourth = lax.all_to_all(fourth, ('sector', 'chan'), 0, 0, tiled=True)  22.2 us
    all_to_all x1, starting transfers between devices, per_device(): fourth = lax.all_to_all(fourth, ('sector', 'chan'), 0, 0, tiled=True)  8.05 us
  transfers between devices with their start and end apart: 8, of which 5 were waited for; matrix products, arithmetic and copies ran while one was open for 17% of the time, Pallas kernels for 0%

profile of v2, /device:TPU:32, one launch (start us, length us, event | category | flops | bytes accessed | tf_op | source)
XLA Modules:
  0.0 192.5 jit_solution(253778882722287001)
XLA Ops:
  6.5 1.8 copy.141
  8.3 1.0 slice.90
  9.7 0.9 constant_dynamic-slice_fusion
  10.9 0.7 copy.84
  11.6 11.2 %all-to-all-start = ((bf16[32,15,128]{2,1,0:T(8,128)(2,1)}), bf16[32,15,128]{2,1,0:T(8,128)(2,1)S(1)}, u32[]{:S(2)}, u32[]{:S(2)}) async-start(bf16[32,15,128]{2,1,0:T(8,128)(2,1)} %copy.84), calls=%async_computation | async-start | bytes 262144 | tf_op jit(solution)/shard_map/all_to_all | solution.py:58
  23.1 0.3 select_reduce_fusion.1
  23.8 8.8 %all-to-all-done = bf16[32,15,128]{2,1,0:T(8,128)(2,1)S(1)} async-done(((bf16[32,15,128]{2,1,0:T(8,128)(2,1)}), bf16[32,15,128]{2,1,0:T(8,128)(2,1)S(1)}, u32[]{:S(2)}, u32[]{:S(2)}) %all-to-all-start) | async-done | bytes 122912 | tf_op jit(solution)/shard_map/all_to_all | solution.py:58
  32.6 0.3 fusion.20
  33.6 0.3 copy.86
  33.9 27.4 %all_to_all.30 = bf16[32,100,128]{2,1,0:T(8,128)(2,1)S(1)} all-to-all(bf16[32,100,128]{2,1,0:T(8,128)(2,1)S(1)} %copy.86), channel_id=1, replica_groups=mesh['sector'=32,'chan'=8] {'sector'}, dimensions={0} | all-to-all | bytes 1638400 | tf_op jit(solution)/shard_map/all_to_all | solution.py:58
  61.7 1.2 reshape.257
  63.0 0.7 select_reduce_fusion.12
  64.6 2.7 %convolution_convert_fusion = bf16[160,16,128]{2,0,1:T(8,128)(2,1)S(1)} fusion(bf16[16,128,640]{2,1,0:T(8,128)(2,1)} %all-gather.6.cloned.1.call-done, bf16[20,8,5,128]{3,2,1,0:T(8,128)(2,1)S(1)} %bitcast.196, pred[640]{0:T(1024)(128)(4,1)S(1)} %iota_compare_fusion.22), kind=kOutput, calls=%fused_computation.7 | convolution fusion | flops 419860480 | bytes 3482240 | tf_op jit(solution)/shard_map/dj,waj->wda/dot_general | solution.py:104
  67.4 1.1 copy.91
  68.5 5.0 %all-to-all-start.2 = ((bf16[32,80,128]{2,1,0:T(8,128)(2,1)}), bf16[32,80,128]{2,1,0:T(8,128)(2,1)S(1)}, u32[]{:S(2)}, u32[]{:S(2)}) async-start(bf16[32,80,128]{2,1,0:T(8,128)(2,1)} %bitcast.40), calls=%async_computation.2 | async-start | bytes 1310720 | tf_op jit(solution)/shard_map/all_to_all | solution.py:58
  73.6 0.6 fusion.90
  74.4 0.3 fusion.49
  74.8 17.9 %all-to-all-done.2 = bf16[32,80,128]{2,1,0:T(8,128)(2,1)S(1)} async-done(((bf16[32,80,128]{2,1,0:T(8,128)(2,1)}), bf16[32,80,128]{2,1,0:T(8,128)(2,1)S(1)}, u32[]{:S(2)}, u32[]{:S(2)}) %all-to-all-start.2) | async-done | bytes 655392 | tf_op jit(solution)/shard_map/all_to_all | solution.py:58
  92.7 0.5 fusion.6
  93.2 1.1 copy.93
  94.3 4.8 %all-to-all-start.3 = ((bf16[32,80,128]{2,1,0:T(8,128)(2,1)}), bf16[32,80,128]{2,1,0:T(8,128)(2,1)S(1)}, u32[]{:S(2)}, u32[]{:S(2)}) async-start(bf16[32,80,128]{2,1,0:T(8,128)(2,1)} %bitcast.49), calls=%async_computation.3 | async-start | bytes 1310720 | tf_op jit(solution)/shard_map/all_to_all | solution.py:58
  99.3 0.9 fusion.48
  100.2 0.9 fusion.47
  101.1 0.4 convolution_select_fusion.2
  101.6 0.4 convolution_select_fusion.1
  101.9 0.4 convolution_select_fusion.3
  102.3 0.4 convolution_select_fusion
  102.8 0.9 reshape.249
  103.7 14.0 %all-to-all-done.3 = bf16[32,80,128]{2,1,0:T(8,128)(2,1)S(1)} async-done(((bf16[32,80,128]{2,1,0:T(8,128)(2,1)}), bf16[32,80,128]{2,1,0:T(8,128)(2,1)S(1)}, u32[]{:S(2)}, u32[]{:S(2)}) %all-to-all-start.3) | async-done | bytes 655392 | tf_op jit(solution)/shard_map/all_to_all | solution.py:58
  117.7 1.7 fusion.29
  119.5 0.8 fusion.91
  120.3 0.5 fusion.27
  120.8 0.8 fusion.13
  121.6 0.5 fusion.25
  122.1 0.8 fusion.17
  122.9 0.5 fusion.23
  123.3 0.8 fusion.18
  124.2 1.5 copy.95
  125.7 8.0 %all-to-all-start.4 = ((bf16[256,2,640]{2,1,0:T(2,128)(2,1)}), bf16[256,2,640]{2,1,0:T(2,128)(2,1)S(1)}, u32[]{:S(2)}, u32[]{:S(2)}) async-start(bf16[256,2,640]{2,1,0:T(2,128)(2,1)} %copy.95), calls=%async_computation.4 | async-start | bytes 1310720 | tf_op jit(solution)/shard_map/all_to_all | solution.py:142
  133.9 22.2 %all-to-all-done.4 = bf16[256,2,640]{2,1,0:T(2,128)(2,1)S(1)} async-done(((bf16[256,2,640]{2,1,0:T(2,128)(2,1)}), bf16[256,2,640]{2,1,0:T(2,128)(2,1)S(1)}, u32[]{:S(2)}, u32[]{:S(2)}) %all-to-all-start.4) | async-done | bytes 655392 | tf_op jit(solution)/shard_map/all_to_all | solution.py:142
  156.1 0.5 reshape.276
  156.6 0.8 fusion.5
  157.4 1.1 copy.98
  158.4 5.6 %all-to-all-start.5 = ((bf16[32,80,128]{2,1,0:T(8,128)(2,1)}), bf16[32,80,128]{2,1,0:T(8,128)(2,1)S(1)}, u32[]{:S(2)}, u32[]{:S(2)}) async-start(bf16[32,80,128]{2,1,0:T(8,128)(2,1)} %bitcast.71), calls=%async_computation.5 | async-start | bytes 1310720 | tf_op jit(solution)/shard_map/all_to_all | solution.py:58
  164.0 3.5 %reshape.250 = bf16[5,8,16,2,640]{4,3,2,1,0:T(2,128)(2,1)S(1)} reshape(bf16[640,1280]{1,0:T(8,128)(2,1)} %all-gather.4.cloned.1.call-done) | data formatting | bytes 3276800 | tf_op jit(solution)/shard_map/reshape | solution.py:149
  167.5 16.5 %all-to-all-done.5 = bf16[32,80,128]{2,1,0:T(8,128)(2,1)S(1)} async-done(((bf16[32,80,128]{2,1,0:T(8,128)(2,1)}), bf16[32,80,128]{2,1,0:T(8,128)(2,1)S(1)}, u32[]{:S(2)}, u32[]{:S(2)}) %all-to-all-start.5) | async-done | bytes 655392 | tf_op jit(solution)/shard_map/all_to_all | solution.py:58
  184.0 0.8 fusion.14
  184.8 1.2 copy.101
  (59 shorter events, 3.7 us)
Async XLA Ops:
  6.5 16.3 %copy-start.3 = (s32[16]{0:T(128)S(1)}, s32[16]{0:T(128)}, u32[]{:S(2)}) copy-start(s32[16]{0:T(128)} %param.6) | copy-start | bytes 196
  6.5 16.5 %copy-start.1 = (s32[2,2,16]{2,1,0:T(2,128)S(1)}, s32[2,2,16]{2,1,0:T(2,128)}, u32[]{:S(2)}) copy-start(s32[2,2,16]{2,1,0:T(2,128)} %param.7) | copy-start | bytes 772
  6.5 58.1 %all-gather.6.cloned.1.call-start = ((), (), s32[]{:S(2)}) async-start(), calls=%async_computation.7 | async-start | bytes 2949120 | tf_op jit(solution)/shard_map/all_gather | solution.py:72
  11.6 21.0 %all-to-all-start = ((bf16[32,15,128]{2,1,0:T(8,128)(2,1)}), bf16[32,15,128]{2,1,0:T(8,128)(2,1)S(1)}, u32[]{:S(2)}, u32[]{:S(2)}) async-start(bf16[32,15,128]{2,1,0:T(8,128)(2,1)} %copy.84), calls=%async_computation | async-start | bytes 262144 | tf_op jit(solution)/shard_map/all_to_all | solution.py:58
  22.7 95.0 %all-gather.8.cloned.1.call-start = ((), (), s32[]{:S(2)}) async-start(), calls=%async_computation.8 | async-start | bytes 3686400 | tf_op jit(solution)/shard_map/all_gather | solution.py:98
  64.6 9.5 %copy-start.2 = (f32[2,2,16,16]{3,2,1,0:T(8,128)S(1)}, f32[2,2,16,16]{3,2,1,0:T(8,128)}, u32[]{:S(2)}) copy-start(f32[2,2,16,16]{3,2,1,0:T(8,128)} %param.9) | copy-start | bytes 12292
  68.5 24.2 %all-to-all-start.2 = ((bf16[32,80,128]{2,1,0:T(8,128)(2,1)}), bf16[32,80,128]{2,1,0:T(8,128)(2,1)S(1)}, u32[]{:S(2)}, u32[]{:S(2)}) async-start(bf16[32,80,128]{2,1,0:T(8,128)(2,1)} %bitcast.40), calls=%async_computation.2 | async-start | bytes 1310720 | tf_op jit(solution)/shard_map/all_to_all | solution.py:58
  94.3 23.4 %all-to-all-start.3 = ((bf16[32,80,128]{2,1,0:T(8,128)(2,1)}), bf16[32,80,128]{2,1,0:T(8,128)(2,1)S(1)}, u32[]{:S(2)}, u32[]{:S(2)}) async-start(bf16[32,80,128]{2,1,0:T(8,128)(2,1)} %bitcast.49), calls=%async_computation.3 | async-start | bytes 1310720 | tf_op jit(solution)/shard_map/all_to_all | solution.py:58
  99.1 64.9 %all-gather.4.cloned.1.call-start = ((), (), s32[]{:S(2)}) async-start(), calls=%async_computation.6 | async-start | bytes 1843200 | tf_op jit(solution)/shard_map/all_gather | solution.py:99
  117.7 2.6 %copy-start = (bf16[640,2560]{1,0:T(8,128)(2,1)S(1)}, bf16[640,2560]{1,0:T(8,128)(2,1)}, u32[]{:S(2)}) copy-start(bf16[640,2560]{1,0:T(8,128)(2,1)} %all-gather.8.cloned.1.call-done) | copy-start | bytes 9830404
  125.7 30.4 %all-to-all-start.4 = ((bf16[256,2,640]{2,1,0:T(2,128)(2,1)}), bf16[256,2,640]{2,1,0:T(2,128)(2,1)S(1)}, u32[]{:S(2)}, u32[]{:S(2)}) async-start(bf16[256,2,640]{2,1,0:T(2,128)(2,1)} %copy.95), calls=%async_computation.4 | async-start | bytes 1310720 | tf_op jit(solution)/shard_map/all_to_all | solution.py:142
  158.4 25.6 %all-to-all-start.5 = ((bf16[32,80,128]{2,1,0:T(8,128)(2,1)}), bf16[32,80,128]{2,1,0:T(8,128)(2,1)S(1)}, u32[]{:S(2)}, u32[]{:S(2)}) async-start(bf16[32,80,128]{2,1,0:T(8,128)(2,1)} %bitcast.71), calls=%async_computation.5 | async-start | bytes 1310720 | tf_op jit(solution)/shard_map/all_to_all | solution.py:58
Sparse Core Ops, SparseCore 0:
  9.2 31.1 all-gather.5
  63.1 27.2 all-gather.7
  103.9 28.2 all-gather.3

commit v3 on v2

--- a/solution.py
+++ b/solution.py
@@ -67,7 +67,7 @@
     fine = TILE // CHANS
     half = tiles // 2
     piece = part // half
-    exact = lax.Precision.HIGHEST
+    exact, fast = lax.Precision.HIGHEST, lax.Precision.HIGH
 
     gathered = lax.all_gather(environment.transpose(1, 0, 2), "chan", axis=0, tiled=True)
 
@@ -80,6 +80,8 @@
 
     own, target, anchor = layout_tables(sector_sizes, joining_table, tiles)
     width = pick(own[1], position) * TILE
+    anchor_width = pick(anchor[1][0], position) * TILE
+    width, anchor_width, spread = lax.optimization_barrier((width, anchor_width, spread))
     mine = sources(*own, tiles).astype(BF16)
     theirs = sources(*target, tiles).astype(BF16)
     theirs = jnp.where(position < half, theirs[:, 0], theirs[:, 1])
@@ -122,14 +124,14 @@
         spread_out = jnp.einsum("rw,qw->rq", spread_out, natural, precision=exact)
         return jnp.where(same, spread_out, 0.0)
 
-    scale0 = 3.0 / (pick(anchor[1][0], position) * TILE).astype(F32)
+    scale0 = 3.0 / anchor_width.astype(F32)
     scale1 = 3.0 / width.astype(F32)
     mixed = jnp.zeros((tiles * CHANS, window), F32)
     for s in range(2):
         second = jnp.dot(
             rows[s], maps_a[:, s * window : (s + 1) * window], preferred_element_type=F32
         )
-        mixed = mixed + jnp.dot(blend(mixing[0, s] * scale0[s], natural), second, precision=exact)
+        mixed = mixed + jnp.dot(blend(mixing[0, s] * scale0[s], natural), second, precision=fast)
     middle = mixed.astype(BF16)
 
     fourth = []
@@ -137,7 +139,7 @@
         third = jnp.dot(
             middle, maps_a[:, s * window : (s + 1) * window], preferred_element_type=F32
         )
-        fourth.append(jnp.dot(blend(mixing[1, s - 2] * scale1, paired), third, precision=exact))
+        fourth.append(jnp.dot(blend(mixing[1, s - 2] * scale1, paired), third, precision=fast))
     fourth = jnp.stack(fourth, axis=1).astype(BF16)
     fourth = lax.all_to_all(fourth, ("sector", "chan"), 0, 0, tiled=True)
     fourth = fourth.reshape(tiles, CHANS, 2, MAXK, TILE).transpose(0, 2, 3, 1, 4)

time: 193 us -> 189 us (0.979)
  waiting for transfers between devices: 79.4 us -> 77.3 us
    all_to_all x4, waiting for transfers between devices: 57.1 us -> 55 us  [deliver(): return lax.all_to_all(blocks, 'sector', 0, 0, tiled=True)]
  transfers between devices with their start and end apart: 8 -> 8, of which waited for: 5 -> 5; matrix products, arithmetic and copies ran while one was open for 17% -> 16% of each run, Pallas kernels for 0% -> 0%
where the time goes in v3:
time: 189 us; the launch traced here: 188 us
  waiting for transfers between devices  77.3 us (41%)
  starting transfers between devices  34.9 us (18%)
  blocking collectives  27.4 us (14%)
  local copies, waits for them, and re-layouts  17.5 us (9%)
  matrix products  14.7 us (8%)
  between operations  14.2 us (8%)
  other arithmetic  2.26 us (1%)
    all_to_all x4, waiting for transfers between devices, deliver(): return lax.all_to_all(blocks, 'sector', 0, 0, tiled=True)  55 us
    all_to_all x1, blocking collectives, deliver(): return lax.all_to_all(blocks, 'sector', 0, 0, tiled=True)  27.4 us
    all_to_all x4, starting transfers between devices, deliver(): return lax.all_to_all(blocks, 'sector', 0, 0, tiled=True)  26.6 us
    all_to_all x1, waiting for transfers between devices, per_device(): fourth = lax.all_to_all(fourth, ('sector', 'chan'), 0, 0, tiled=True)  22.2 us
    all_to_all x1, starting transfers between devices, per_device(): fourth = lax.all_to_all(fourth, ('sector', 'chan'), 0, 0, tiled=True)  8 us
  transfers between devices with their start and end apart: 8, of which 5 were waited for; matrix products, arithmetic and copies ran while one was open for 16% of the time, Pallas kernels for 0%

profile of v3, /device:TPU:32, one launch (start us, length us, event | category | flops | bytes accessed | tf_op | source)
XLA Modules:
  0.0 188.2 jit_solution(18179084382761838755)
XLA Ops:
  6.5 1.0 slice.91
  7.9 0.9 constant_dynamic-slice_fusion
  9.1 0.7 copy.84
  9.8 11.2 %all-to-all-start = ((bf16[32,15,128]{2,1,0:T(8,128)(2,1)}), bf16[32,15,128]{2,1,0:T(8,128)(2,1)S(1)}, u32[]{:S(2)}, u32[]{:S(2)}) async-start(bf16[32,15,128]{2,1,0:T(8,128)(2,1)} %copy.84), calls=%async_computation | async-start | bytes 262144 | tf_op jit(solution)/shard_map/all_to_all | solution.py:58
  21.1 0.8 copy.141
  22.0 0.3 select_reduce_fusion.1
  23.0 0.6 select_reduce_fusion.12
  24.2 6.6 %all-to-all-done = bf16[32,15,128]{2,1,0:T(8,128)(2,1)S(1)} async-done(((bf16[32,15,128]{2,1,0:T(8,128)(2,1)}), bf16[32,15,128]{2,1,0:T(8,128)(2,1)S(1)}, u32[]{:S(2)}, u32[]{:S(2)}) %all-to-all-start) | async-done | bytes 122912 | tf_op jit(solution)/shard_map/all_to_all | solution.py:58
  30.8 0.3 fusion.20
  31.9 0.3 copy.86
  32.2 27.4 %all_to_all.30 = bf16[32,100,128]{2,1,0:T(8,128)(2,1)S(1)} all-to-all(bf16[32,100,128]{2,1,0:T(8,128)(2,1)S(1)} %copy.86), channel_id=1, replica_groups=mesh['sector'=32,'chan'=8] {'sector'}, dimensions={0} | all-to-all | bytes 1638400 | tf_op jit(solution)/shard_map/all_to_all | solution.py:58
  60.0 1.2 reshape.257
  61.5 2.8 %convolution_convert_fusion = bf16[160,16,128]{2,0,1:T(8,128)(2,1)S(1)} fusion(bf16[16,128,640]{2,1,0:T(8,128)(2,1)} %all-gather.6.cloned.1.call-done, bf16[20,8,5,128]{3,2,1,0:T(8,128)(2,1)S(1)} %bitcast.197, pred[640]{0:T(1024)(128)(4,1)S(1)} %iota_compare_fusion.22), kind=kOutput, calls=%fused_computation.7 | convolution fusion | flops 419860480 | bytes 3482240 | tf_op jit(solution)/shard_map/dj,waj->wda/dot_general | solution.py:106
  64.2 1.1 copy.91
  65.3 5.0 %all-to-all-start.2 = ((bf16[32,80,128]{2,1,0:T(8,128)(2,1)}), bf16[32,80,128]{2,1,0:T(8,128)(2,1)S(1)}, u32[]{:S(2)}, u32[]{:S(2)}) async-start(bf16[32,80,128]{2,1,0:T(8,128)(2,1)} %bitcast.40), calls=%async_computation.2 | async-start | bytes 1310720 | tf_op jit(solution)/shard_map/all_to_all | solution.py:58
  70.5 0.6 fusion.98
  71.3 0.3 fusion.49
  71.6 18.0 %all-to-all-done.2 = bf16[32,80,128]{2,1,0:T(8,128)(2,1)S(1)} async-done(((bf16[32,80,128]{2,1,0:T(8,128)(2,1)}), bf16[32,80,128]{2,1,0:T(8,128)(2,1)S(1)}, u32[]{:S(2)}, u32[]{:S(2)}) %all-to-all-start.2) | async-done | bytes 655392 | tf_op jit(solution)/shard_map/all_to_all | solution.py:58
  89.5 0.5 fusion.6
  90.0 1.1 copy.93
  91.1 4.8 %all-to-all-start.3 = ((bf16[32,80,128]{2,1,0:T(8,128)(2,1)}), bf16[32,80,128]{2,1,0:T(8,128)(2,1)S(1)}, u32[]{:S(2)}, u32[]{:S(2)}) async-start(bf16[32,80,128]{2,1,0:T(8,128)(2,1)} %bitcast.49), calls=%async_computation.3 | async-start | bytes 1310720 | tf_op jit(solution)/shard_map/all_to_all | solution.py:58
  96.2 0.9 fusion.48
  97.1 0.9 fusion.47
  98.0 0.4 convolution_select_fusion.2
  98.4 0.4 convolution_select_fusion.1
  98.8 0.4 convolution_select_fusion.3
  99.1 0.4 convolution_select_fusion
  99.6 0.9 reshape.249
  100.6 14.0 %all-to-all-done.3 = bf16[32,80,128]{2,1,0:T(8,128)(2,1)S(1)} async-done(((bf16[32,80,128]{2,1,0:T(8,128)(2,1)}), bf16[32,80,128]{2,1,0:T(8,128)(2,1)S(1)}, u32[]{:S(2)}, u32[]{:S(2)}) %all-to-all-start.3) | async-done | bytes 655392 | tf_op jit(solution)/shard_map/all_to_all | solution.py:58
  114.6 1.7 fusion.29
  116.3 0.5 fusion.99
  116.9 0.5 fusion.27
  117.3 0.5 fusion.13
  117.9 0.5 fusion.25
  118.3 0.5 fusion.17
  118.9 0.5 fusion.23
  119.3 0.5 fusion.18
  120.0 1.5 copy.95
  121.5 8.0 %all-to-all-start.4 = ((bf16[256,2,640]{2,1,0:T(2,128)(2,1)}), bf16[256,2,640]{2,1,0:T(2,128)(2,1)S(1)}, u32[]{:S(2)}, u32[]{:S(2)}) async-start(bf16[256,2,640]{2,1,0:T(2,128)(2,1)} %copy.95), calls=%async_computation.4 | async-start | bytes 1310720 | tf_op jit(solution)/shard_map/all_to_all | solution.py:144
  129.6 22.2 %all-to-all-done.4 = bf16[256,2,640]{2,1,0:T(2,128)(2,1)S(1)} async-done(((bf16[256,2,640]{2,1,0:T(2,128)(2,1)}), bf16[256,2,640]{2,1,0:T(2,128)(2,1)S(1)}, u32[]{:S(2)}, u32[]{:S(2)}) %all-to-all-start.4) | async-done | bytes 655392 | tf_op jit(solution)/shard_map/all_to_all | solution.py:144
  151.8 0.5 reshape.276
  152.2 0.8 fusion.5
  153.0 1.1 copy.98
  154.1 5.6 %all-to-all-start.5 = ((bf16[32,80,128]{2,1,0:T(8,128)(2,1)}), bf16[32,80,128]{2,1,0:T(8,128)(2,1)S(1)}, u32[]{:S(2)}, u32[]{:S(2)}) async-start(bf16[32,80,128]{2,1,0:T(8,128)(2,1)} %bitcast.71), calls=%async_computation.5 | async-start | bytes 1310720 | tf_op jit(solution)/shard_map/all_to_all | solution.py:58
  159.7 3.5 %reshape.250 = bf16[5,8,16,2,640]{4,3,2,1,0:T(2,128)(2,1)S(1)} reshape(bf16[640,1280]{1,0:T(8,128)(2,1)} %all-gather.4.cloned.1.call-done) | data formatting | bytes 3276800 | tf_op jit(solution)/shard_map/reshape | solution.py:151
  163.2 16.5 %all-to-all-done.5 = bf16[32,80,128]{2,1,0:T(8,128)(2,1)S(1)} async-done(((bf16[32,80,128]{2,1,0:T(8,128)(2,1)}), bf16[32,80,128]{2,1,0:T(8,128)(2,1)S(1)}, u32[]{:S(2)}, u32[]{:S(2)}) %all-to-all-start.5) | async-done | bytes 655392 | tf_op jit(solution)/shard_map/all_to_all | solution.py:58
  179.7 0.8 fusion.14
  180.5 1.2 copy.101
  (62 shorter events, 3.7 us)
Async XLA Ops:
  6.5 14.5 %copy-start.1 = (bf16[128,2,640]{2,1,0:T(2,128)(2,1)S(1)}, bf16[128,2,640]{2,1,0:T(2,128)(2,1)}, u32[]{:S(2)}) copy-start(bf16[128,2,640]{2,1,0:T(2,128)(2,1)} %param.5) | copy-start | bytes 983044
  6.5 15.4 %copy-start.4 = (s32[16]{0:T(128)S(1)}, s32[16]{0:T(128)}, u32[]{:S(2)}) copy-start(s32[16]{0:T(128)} %param.6) | copy-start | bytes 196
  6.5 15.5 %copy-start.2 = (s32[2,2,16]{2,1,0:T(2,128)S(1)}, s32[2,2,16]{2,1,0:T(2,128)}, u32[]{:S(2)}) copy-start(s32[2,2,16]{2,1,0:T(2,128)} %param.7) | copy-start | bytes 772
  9.8 21.0 %all-to-all-start = ((bf16[32,15,128]{2,1,0:T(8,128)(2,1)}), bf16[32,15,128]{2,1,0:T(8,128)(2,1)S(1)}, u32[]{:S(2)}, u32[]{:S(2)}) async-start(bf16[32,15,128]{2,1,0:T(8,128)(2,1)} %copy.84), calls=%async_computation | async-start | bytes 262144 | tf_op jit(solution)/shard_map/all_to_all | solution.py:58
  21.0 40.4 %all-gather.6.cloned.1.call-start = ((), (), s32[]{:S(2)}) async-start(), calls=%async_computation.7 | async-start | bytes 2949120 | tf_op jit(solution)/shard_map/all_gather | solution.py:72
  21.9 92.7 %all-gather.8.cloned.1.call-start = ((), (), s32[]{:S(2)}) async-start(), calls=%async_computation.8 | async-start | bytes 3686400 | tf_op jit(solution)/shard_map/all_gather | solution.py:100
  61.5 9.7 %copy-start.3 = (f32[2,2,16,16]{3,2,1,0:T(8,128)S(1)}, f32[2,2,16,16]{3,2,1,0:T(8,128)}, u32[]{:S(2)}) copy-start(f32[2,2,16,16]{3,2,1,0:T(8,128)} %param.9) | copy-start | bytes 12292
  65.3 24.2 %all-to-all-start.2 = ((bf16[32,80,128]{2,1,0:T(8,128)(2,1)}), bf16[32,80,128]{2,1,0:T(8,128)(2,1)S(1)}, u32[]{:S(2)}, u32[]{:S(2)}) async-start(bf16[32,80,128]{2,1,0:T(8,128)(2,1)} %bitcast.40), calls=%async_computation.2 | async-start | bytes 1310720 | tf_op jit(solution)/shard_map/all_to_all | solution.py:58
  91.1 23.4 %all-to-all-start.3 = ((bf16[32,80,128]{2,1,0:T(8,128)(2,1)}), bf16[32,80,128]{2,1,0:T(8,128)(2,1)S(1)}, u32[]{:S(2)}, u32[]{:S(2)}) async-start(bf16[32,80,128]{2,1,0:T(8,128)(2,1)} %bitcast.49), calls=%async_computation.3 | async-start | bytes 1310720 | tf_op jit(solution)/shard_map/all_to_all | solution.py:58
  95.9 63.8 %all-gather.4.cloned.1.call-start = ((), (), s32[]{:S(2)}) async-start(), calls=%async_computation.6 | async-start | bytes 1843200 | tf_op jit(solution)/shard_map/all_gather | solution.py:101
  114.6 2.3 %copy-start = (bf16[640,2560]{1,0:T(8,128)(2,1)S(1)}, bf16[640,2560]{1,0:T(8,128)(2,1)}, u32[]{:S(2)}) copy-start(bf16[640,2560]{1,0:T(8,128)(2,1)} %all-gather.8.cloned.1.call-done) | copy-start | bytes 9830404
  121.5 30.3 %all-to-all-start.4 = ((bf16[256,2,640]{2,1,0:T(2,128)(2,1)}), bf16[256,2,640]{2,1,0:T(2,128)(2,1)S(1)}, u32[]{:S(2)}, u32[]{:S(2)}) async-start(bf16[256,2,640]{2,1,0:T(2,128)(2,1)} %copy.95), calls=%async_computation.4 | async-start | bytes 1310720 | tf_op jit(solution)/shard_map/all_to_all | solution.py:144
  154.1 25.6 %all-to-all-start.5 = ((bf16[32,80,128]{2,1,0:T(8,128)(2,1)}), bf16[32,80,128]{2,1,0:T(8,128)(2,1)S(1)}, u32[]{:S(2)}, u32[]{:S(2)}) async-start(bf16[32,80,128]{2,1,0:T(8,128)(2,1)} %bitcast.71), calls=%async_computation.5 | async-start | bytes 1310720 | tf_op jit(solution)/shard_map/all_to_all | solution.py:58
Sparse Core Ops, SparseCore 0:
  23.6 29.7 all-gather.5
  61.3 27.2 all-gather.7
  100.7 28.2 all-gather.3

commit v4 on v3

--- a/solution.py
+++ b/solution.py
@@ -71,8 +71,8 @@
 
     gathered = lax.all_gather(environment.transpose(1, 0, 2), "chan", axis=0, tiled=True)
 
-    slim = lax.dynamic_slice_in_dim(isometry[0], chan * fine, fine, 2)
-    slim = slim.transpose(0, 2, 1).reshape(2, part, TILE)
+    slim = lax.dynamic_slice(isometry, (0, 0, 0, chan * fine), (1, 2, window, fine))
+    slim = slim[0].transpose(0, 2, 1).reshape(2, part, TILE)
     slices = lax.dynamic_slice_in_dim(isometry, chan * part, part, 2)
     kinds = jnp.concatenate([slim[None], slices])
     kinds = kinds.reshape(3, tiles, piece, TILE).transpose(1, 0, 2, 3)

time: 189 us -> 188 us (level)
  no operation moved by 1% of the time
where the time goes in v4:
time: 188 us; the launch traced here: 187 us
  waiting for transfers between devices  77.3 us (41%)
  starting transfers between devices  34.9 us (19%)
  blocking collectives  27.4 us (15%)
  local copies, waits for them, and re-layouts  16.6 us (9%)
  matrix products  14.7 us (8%)
  between operations  14.2 us (8%)
  other arithmetic  2.26 us (1%)
    all_to_all x4, waiting for transfers between devices, deliver(): return lax.all_to_all(blocks, 'sector', 0, 0, tiled=True)  55 us
    all_to_all x1, blocking collectives, deliver(): return lax.all_to_all(blocks, 'sector', 0, 0, tiled=True)  27.4 us
    all_to_all x4, starting transfers between devices, deliver(): return lax.all_to_all(blocks, 'sector', 0, 0, tiled=True)  26.6 us
    all_to_all x1, waiting for transfers between devices, per_device(): fourth = lax.all_to_all(fourth, ('sector', 'chan'), 0, 0, tiled=True)  22.2 us
    all_to_all x1, starting transfers between devices, per_device(): fourth = lax.all_to_all(fourth, ('sector', 'chan'), 0, 0, tiled=True)  8 us
  transfers between devices with their start and end apart: 8, of which 5 were waited for; matrix products, arithmetic and copies ran while one was open for 16% of the time, Pallas kernels for 0%

profile of v4, /device:TPU:32, one launch (start us, length us, event | category | flops | bytes accessed | tf_op | source)
XLA Modules:
  0.0 187.4 jit_solution(359685272346558527)
XLA Ops:
  6.5 1.1 copy-done
  8.3 0.7 copy.84
  9.0 11.2 %all-to-all-start = ((bf16[32,15,128]{2,1,0:T(8,128)(2,1)}), bf16[32,15,128]{2,1,0:T(8,128)(2,1)S(1)}, u32[]{:S(2)}, u32[]{:S(2)}) async-start(bf16[32,15,128]{2,1,0:T(8,128)(2,1)} %copy.84), calls=%async_computation | async-start | bytes 262144 | tf_op jit(solution)/shard_map/all_to_all | solution.py:58
  20.2 0.8 copy.140
  21.2 0.3 select_reduce_fusion.1
  22.1 0.6 select_reduce_fusion.12
  23.4 6.6 %all-to-all-done = bf16[32,15,128]{2,1,0:T(8,128)(2,1)S(1)} async-done(((bf16[32,15,128]{2,1,0:T(8,128)(2,1)}), bf16[32,15,128]{2,1,0:T(8,128)(2,1)S(1)}, u32[]{:S(2)}, u32[]{:S(2)}) %all-to-all-start) | async-done | bytes 122912 | tf_op jit(solution)/shard_map/all_to_all | solution.py:58
  30.0 0.3 fusion.20
  30.3 0.3 fusion.22
  31.0 0.3 copy.86
  31.4 27.4 %all_to_all.30 = bf16[32,100,128]{2,1,0:T(8,128)(2,1)S(1)} all-to-all(bf16[32,100,128]{2,1,0:T(8,128)(2,1)S(1)} %copy.86), channel_id=1, replica_groups=mesh['sector'=32,'chan'=8] {'sector'}, dimensions={0} | all-to-all | bytes 1638400 | tf_op jit(solution)/shard_map/all_to_all | solution.py:58
  59.1 1.2 reshape.256
  60.6 2.8 %convolution_convert_fusion = bf16[160,16,128]{2,0,1:T(8,128)(2,1)S(1)} fusion(bf16[16,128,640]{2,1,0:T(8,128)(2,1)} %all-gather.6.cloned.1.call-done, bf16[20,8,5,128]{3,2,1,0:T(8,128)(2,1)S(1)} %bitcast.197, pred[640]{0:T(1024)(128)(4,1)S(1)} %iota_compare_fusion.22), kind=kOutput, calls=%fused_computation.7 | convolution fusion | flops 419860480 | bytes 3482240 | tf_op jit(solution)/shard_map/dj,waj->wda/dot_general | solution.py:106
  63.4 1.1 copy.91
  64.5 5.0 %all-to-all-start.2 = ((bf16[32,80,128]{2,1,0:T(8,128)(2,1)}), bf16[32,80,128]{2,1,0:T(8,128)(2,1)S(1)}, u32[]{:S(2)}, u32[]{:S(2)}) async-start(bf16[32,80,128]{2,1,0:T(8,128)(2,1)} %bitcast.40), calls=%async_computation.2 | async-start | bytes 1310720 | tf_op jit(solution)/shard_map/all_to_all | solution.py:58
  69.7 0.6 fusion.98
  70.5 0.3 fusion.49
  70.8 18.0 %all-to-all-done.2 = bf16[32,80,128]{2,1,0:T(8,128)(2,1)S(1)} async-done(((bf16[32,80,128]{2,1,0:T(8,128)(2,1)}), bf16[32,80,128]{2,1,0:T(8,128)(2,1)S(1)}, u32[]{:S(2)}, u32[]{:S(2)}) %all-to-all-start.2) | async-done | bytes 655392 | tf_op jit(solution)/shard_map/all_to_all | solution.py:58
  88.7 0.5 fusion.6
  89.2 1.1 copy.93
  90.3 4.8 %all-to-all-start.3 = ((bf16[32,80,128]{2,1,0:T(8,128)(2,1)}), bf16[32,80,128]{2,1,0:T(8,128)(2,1)S(1)}, u32[]{:S(2)}, u32[]{:S(2)}) async-start(bf16[32,80,128]{2,1,0:T(8,128)(2,1)} %bitcast.49), calls=%async_computation.3 | async-start | bytes 1310720 | tf_op jit(solution)/shard_map/all_to_all | solution.py:58
  95.3 0.9 fusion.48
  96.2 0.9 fusion.47
  97.1 0.4 convolution_select_fusion.2
  97.6 0.4 convolution_select_fusion.1
  97.9 0.4 convolution_select_fusion.3
  98.3 0.4 convolution_select_fusion
  98.8 0.9 reshape.248
  99.7 14.0 %all-to-all-done.3 = bf16[32,80,128]{2,1,0:T(8,128)(2,1)S(1)} async-done(((bf16[32,80,128]{2,1,0:T(8,128)(2,1)}), bf16[32,80,128]{2,1,0:T(8,128)(2,1)S(1)}, u32[]{:S(2)}, u32[]{:S(2)}) %all-to-all-start.3) | async-done | bytes 655392 | tf_op jit(solution)/shard_map/all_to_all | solution.py:58
  113.7 1.7 fusion.29
  115.5 0.5 fusion.99
  116.0 0.5 fusion.27
  116.5 0.5 fusion.13
  117.0 0.5 fusion.25
  117.5 0.5 fusion.17
  118.0 0.5 fusion.23
  118.5 0.5 fusion.18
  119.1 1.5 copy.95
  120.6 8.0 %all-to-all-start.4 = ((bf16[256,2,640]{2,1,0:T(2,128)(2,1)}), bf16[256,2,640]{2,1,0:T(2,128)(2,1)S(1)}, u32[]{:S(2)}, u32[]{:S(2)}) async-start(bf16[256,2,640]{2,1,0:T(2,128)(2,1)} %copy.95), calls=%async_computation.4 | async-start | bytes 1310720 | tf_op jit(solution)/shard_map/all_to_all | solution.py:144
  128.8 22.2 %all-to-all-done.4 = bf16[256,2,640]{2,1,0:T(2,128)(2,1)S(1)} async-done(((bf16[256,2,640]{2,1,0:T(2,128)(2,1)}), bf16[256,2,640]{2,1,0:T(2,128)(2,1)S(1)}, u32[]{:S(2)}, u32[]{:S(2)}) %all-to-all-start.4) | async-done | bytes 655392 | tf_op jit(solution)/shard_map/all_to_all | solution.py:144
  151.0 0.5 reshape.275
  151.4 0.8 fusion.5
  152.2 1.1 copy.98
  153.3 5.6 %all-to-all-start.5 = ((bf16[32,80,128]{2,1,0:T(8,128)(2,1)}), bf16[32,80,128]{2,1,0:T(8,128)(2,1)S(1)}, u32[]{:S(2)}, u32[]{:S(2)}) async-start(bf16[32,80,128]{2,1,0:T(8,128)(2,1)} %bitcast.71), calls=%async_computation.5 | async-start | bytes 1310720 | tf_op jit(solution)/shard_map/all_to_all | solution.py:58
  158.9 3.5 %reshape.249 = bf16[5,8,16,2,640]{4,3,2,1,0:T(2,128)(2,1)S(1)} reshape(bf16[640,1280]{1,0:T(8,128)(2,1)} %all-gather.4.cloned.1.call-done) | data formatting | bytes 3276800 | tf_op jit(solution)/shard_map/reshape | solution.py:151
  162.4 16.5 %all-to-all-done.5 = bf16[32,80,128]{2,1,0:T(8,128)(2,1)S(1)} async-done(((bf16[32,80,128]{2,1,0:T(8,128)(2,1)}), bf16[32,80,128]{2,1,0:T(8,128)(2,1)S(1)}, u32[]{:S(2)}, u32[]{:S(2)}) %all-to-all-start.5) | async-done | bytes 655392 | tf_op jit(solution)/shard_map/all_to_all | solution.py:58
  178.9 0.8 fusion.14
  179.7 1.2 copy.101
  (63 shorter events, 3.4 us)
Async XLA Ops:
  6.5 1.1 copy-start
  6.5 13.7 %copy-start.2 = (bf16[128,2,640]{2,1,0:T(2,128)(2,1)S(1)}, bf16[128,2,640]{2,1,0:T(2,128)(2,1)}, u32[]{:S(2)}) copy-start(bf16[128,2,640]{2,1,0:T(2,128)(2,1)} %param.5) | copy-start | bytes 983044
  6.5 14.5 %copy-start.5 = (s32[16]{0:T(128)S(1)}, s32[16]{0:T(128)}, u32[]{:S(2)}) copy-start(s32[16]{0:T(128)} %param.6) | copy-start | bytes 196
  6.5 14.7 %copy-start.3 = (s32[2,2,16]{2,1,0:T(2,128)S(1)}, s32[2,2,16]{2,1,0:T(2,128)}, u32[]{:S(2)}) copy-start(s32[2,2,16]{2,1,0:T(2,128)} %param.7) | copy-start | bytes 772
  9.0 21.0 %all-to-all-start = ((bf16[32,15,128]{2,1,0:T(8,128)(2,1)}), bf16[32,15,128]{2,1,0:T(8,128)(2,1)S(1)}, u32[]{:S(2)}, u32[]{:S(2)}) async-start(bf16[32,15,128]{2,1,0:T(8,128)(2,1)} %copy.84), calls=%async_computation | async-start | bytes 262144 | tf_op jit(solution)/shard_map/all_to_all | solution.py:58
  20.2 40.4 %all-gather.6.cloned.1.call-start = ((), (), s32[]{:S(2)}) async-start(), calls=%async_computation.7 | async-start | bytes 2949120 | tf_op jit(solution)/shard_map/all_gather | solution.py:72
  21.0 92.7 %all-gather.8.cloned.1.call-start = ((), (), s32[]{:S(2)}) async-start(), calls=%async_computation.8 | async-start | bytes 3686400 | tf_op jit(solution)/shard_map/all_gather | solution.py:100
  60.6 9.7 %copy-start.4 = (f32[2,2,16,16]{3,2,1,0:T(8,128)S(1)}, f32[2,2,16,16]{3,2,1,0:T(8,128)}, u32[]{:S(2)}) copy-start(f32[2,2,16,16]{3,2,1,0:T(8,128)} %param.9) | copy-start | bytes 12292
  64.5 24.2 %all-to-all-start.2 = ((bf16[32,80,128]{2,1,0:T(8,128)(2,1)}), bf16[32,80,128]{2,1,0:T(8,128)(2,1)S(1)}, u32[]{:S(2)}, u32[]{:S(2)}) async-start(bf16[32,80,128]{2,1,0:T(8,128)(2,1)} %bitcast.40), calls=%async_computation.2 | async-start | bytes 1310720 | tf_op jit(solution)/shard_map/all_to_all | solution.py:58
  90.3 23.4 %all-to-all-start.3 = ((bf16[32,80,128]{2,1,0:T(8,128)(2,1)}), bf16[32,80,128]{2,1,0:T(8,128)(2,1)S(1)}, u32[]{:S(2)}, u32[]{:S(2)}) async-start(bf16[32,80,128]{2,1,0:T(8,128)(2,1)} %bitcast.49), calls=%async_computation.3 | async-start | bytes 1310720 | tf_op jit(solution)/shard_map/all_to_all | solution.py:58
  95.1 63.8 %all-gather.4.cloned.1.call-start = ((), (), s32[]{:S(2)}) async-start(), calls=%async_computation.6 | async-start | bytes 1843200 | tf_op jit(solution)/shard_map/all_gather | solution.py:101
  113.7 2.3 %copy-start.1 = (bf16[640,2560]{1,0:T(8,128)(2,1)S(1)}, bf16[640,2560]{1,0:T(8,128)(2,1)}, u32[]{:S(2)}) copy-start(bf16[640,2560]{1,0:T(8,128)(2,1)} %all-gather.8.cloned.1.call-done) | copy-start | bytes 9830404
  120.6 30.3 %all-to-all-start.4 = ((bf16[256,2,640]{2,1,0:T(2,128)(2,1)}), bf16[256,2,640]{2,1,0:T(2,128)(2,1)S(1)}, u32[]{:S(2)}, u32[]{:S(2)}) async-start(bf16[256,2,640]{2,1,0:T(2,128)(2,1)} %copy.95), calls=%async_computation.4 | async-start | bytes 1310720 | tf_op jit(solution)/shard_map/all_to_all | solution.py:144
  153.3 25.6 %all-to-all-start.5 = ((bf16[32,80,128]{2,1,0:T(8,128)(2,1)}), bf16[32,80,128]{2,1,0:T(8,128)(2,1)S(1)}, u32[]{:S(2)}, u32[]{:S(2)}) async-start(bf16[32,80,128]{2,1,0:T(8,128)(2,1)} %bitcast.71), calls=%async_computation.5 | async-start | bytes 1310720 | tf_op jit(solution)/shard_map/all_to_all | solution.py:58
Sparse Core Ops, SparseCore 0:
  22.8 29.7 all-gather.5
  60.5 27.2 all-gather.7
  99.9 28.2 all-gather.3

commit v5 on v4

--- a/solution.py
+++ b/solution.py
@@ -107,6 +107,8 @@
     first = first.reshape(2, CHANS, 2 * MAXK, fine, TILE).transpose(3, 0, 2, 1, 4)
     first = deliver(first.reshape(tiles, 2 * MAXK * CHANS, TILE))
     select0 = selection(own[0], (anchor[0][0], anchor[1][0]), tiles)
+    select1 = selection(own[0], (anchor[0][1], anchor[1][1]), tiles)
+    first, select1 = lax.optimization_barrier((first, select1))
     first = route(select0, first.reshape(tiles, 2, MAXK, CHANS, TILE))
     first = deliver(first.reshape(tiles, 2 * MAXK * CHANS, TILE))
     rows = first.reshape(tiles, 2, MAXK, CHANS, TILE).transpose(1, 0, 3, 2, 4)
@@ -143,7 +145,6 @@
     fourth = jnp.stack(fourth, axis=1).astype(BF16)
     fourth = lax.all_to_all(fourth, ("sector", "chan"), 0, 0, tiled=True)
     fourth = fourth.reshape(tiles, CHANS, 2, MAXK, TILE).transpose(0, 2, 3, 1, 4)
-    select1 = selection(own[0], (anchor[0][1], anchor[1][1]), tiles)
     fourth = deliver(route(select1, fourth).reshape(tiles, 2 * MAXK * CHANS, TILE))
     result = jnp.einsum(
         "jvsicb,icjsd->bvd",

time: 188 us -> 187 us (level)
  blocking collectives: 27.4 us -> 57.5 us
  waiting for transfers between devices: 77.3 us -> 55 us
  starting transfers between devices: 34.9 us -> 26.9 us
    all_to_all x0 -> x1, blocking collectives: none -> 30.1 us  [per_device(): fourth = lax.all_to_all(fourth, ('sector', 'chan'), 0, 0, tiled=True)]
    all_to_all x1 -> x0, waiting for transfers between devices: 22.2 us -> none  [per_device(): fourth = lax.all_to_all(fourth, ('sector', 'chan'), 0, 0, tiled=True)]
    all_to_all x1 -> x0, starting transfers between devices: 8 us -> none  [per_device(): fourth = lax.all_to_all(fourth, ('sector', 'chan'), 0, 0, tiled=True)]
  transfers between devices with their start and end apart: 8 -> 7, of which waited for: 5 -> 4; matrix products, arithmetic and copies ran while one was open for 16% -> 15% of each run, Pallas kernels for 0% -> 0%
where the time goes in v5:
time: 187 us; the launch traced here: 186 us
  blocking collectives  57.5 us (31%)
  waiting for transfers between devices  55 us (29%)
  starting transfers between devices  26.9 us (14%)
  local copies, waits for them, and re-layouts  15.8 us (8%)
  matrix products  14.7 us (8%)
  between operations  14.2 us (8%)
  other arithmetic  2.41 us (1%)
    all_to_all x4, waiting for transfers between devices, deliver(): return lax.all_to_all(blocks, 'sector', 0, 0, tiled=True)  54.9 us
    all_to_all x1, blocking collectives, per_device(): fourth = lax.all_to_all(fourth, ('sector', 'chan'), 0, 0, tiled=True)  30.1 us
    all_to_all x1, blocking collectives, deliver(): return lax.all_to_all(blocks, 'sector', 0, 0, tiled=True)  27.4 us
    all_to_all x4, starting transfers between devices, deliver(): return lax.all_to_all(blocks, 'sector', 0, 0, tiled=True)  26.5 us
  transfers between devices with their start and end apart: 7, of which 4 were waited for; matrix products, arithmetic and copies ran while one was open for 15% of the time, Pallas kernels for 0%

profile of v5, /device:TPU:32, one launch (start us, length us, event | category | flops | bytes accessed | tf_op | source)
XLA Modules:
  0.0 186.4 jit_solution(11829165597034466676)
XLA Ops:
  6.5 1.1 copy-done
  8.3 0.7 copy.84
  9.0 11.2 %all-to-all-start = ((bf16[32,15,128]{2,1,0:T(8,128)(2,1)}), bf16[32,15,128]{2,1,0:T(8,128)(2,1)S(1)}, u32[]{:S(2)}, u32[]{:S(2)}) async-start(bf16[32,15,128]{2,1,0:T(8,128)(2,1)} %copy.84), calls=%async_computation | async-start | bytes 262144 | tf_op jit(solution)/shard_map/all_to_all | solution.py:58
  20.2 0.8 copy.140
  21.2 0.3 select_reduce_fusion.1
  22.1 0.6 select_reduce_fusion.12
  23.4 6.6 %all-to-all-done = bf16[32,15,128]{2,1,0:T(8,128)(2,1)S(1)} async-done(((bf16[32,15,128]{2,1,0:T(8,128)(2,1)}), bf16[32,15,128]{2,1,0:T(8,128)(2,1)S(1)}, u32[]{:S(2)}, u32[]{:S(2)}) %all-to-all-start) | async-done | bytes 122912 | tf_op jit(solution)/shard_map/all_to_all | solution.py:58
  30.0 0.3 fusion.20
  30.3 0.3 fusion.22
  31.0 0.3 copy.86
  31.4 27.4 %all_to_all.30 = bf16[32,100,128]{2,1,0:T(8,128)(2,1)S(1)} all-to-all(bf16[32,100,128]{2,1,0:T(8,128)(2,1)S(1)} %copy.86), channel_id=1, replica_groups=mesh['sector'=32,'chan'=8] {'sector'}, dimensions={0} | all-to-all | bytes 1638400 | tf_op jit(solution)/shard_map/all_to_all | solution.py:58
  59.1 1.2 reshape.256
  60.8 2.8 %convolution_convert_fusion = bf16[160,16,128]{2,0,1:T(8,128)(2,1)S(1)} fusion(bf16[16,128,640]{2,1,0:T(8,128)(2,1)} %all-gather.6.cloned.1.call-done, bf16[20,8,5,128]{3,2,1,0:T(8,128)(2,1)S(1)} %bitcast.197, pred[640]{0:T(1024)(128)(4,1)S(1)} %iota_compare_fusion.22), kind=kOutput, calls=%fused_computation.7 | convolution fusion | flops 419860480 | bytes 3482240 | tf_op jit(solution)/shard_map/dj,waj->wda/dot_general | solution.py:106
  63.5 1.1 copy.91
  64.6 5.0 %all-to-all-start.2 = ((bf16[32,80,128]{2,1,0:T(8,128)(2,1)}), bf16[32,80,128]{2,1,0:T(8,128)(2,1)S(1)}, u32[]{:S(2)}, u32[]{:S(2)}) async-start(bf16[32,80,128]{2,1,0:T(8,128)(2,1)} %bitcast.40), calls=%async_computation.2 | async-start | bytes 1310720 | tf_op jit(solution)/shard_map/all_to_all | solution.py:58
  70.0 0.6 fusion.95
  70.8 0.3 fusion.46
  71.0 17.8 %all-to-all-done.2 = bf16[32,80,128]{2,1,0:T(8,128)(2,1)S(1)} async-done(((bf16[32,80,128]{2,1,0:T(8,128)(2,1)}), bf16[32,80,128]{2,1,0:T(8,128)(2,1)S(1)}, u32[]{:S(2)}, u32[]{:S(2)}) %all-to-all-start.2) | async-done | bytes 655392 | tf_op jit(solution)/shard_map/all_to_all | solution.py:58
  88.8 0.5 fusion.6
  89.3 1.1 copy.93
  90.4 4.8 %all-to-all-start.3 = ((bf16[32,80,128]{2,1,0:T(8,128)(2,1)}), bf16[32,80,128]{2,1,0:T(8,128)(2,1)S(1)}, u32[]{:S(2)}, u32[]{:S(2)}) async-start(bf16[32,80,128]{2,1,0:T(8,128)(2,1)} %bitcast.51), calls=%async_computation.3 | async-start | bytes 1310720 | tf_op jit(solution)/shard_map/all_to_all | solution.py:58
  95.2 0.2 all-gather.4.cloned.1.call-start
  95.5 0.9 fusion.45
  96.4 0.9 fusion.44
  97.3 0.4 convolution_select_fusion.2
  97.7 0.4 convolution_select_fusion.1
  98.1 0.4 convolution_select_fusion.3
  98.5 0.4 convolution_select_fusion
  98.9 0.9 reshape.248
  99.9 14.0 %all-to-all-done.3 = bf16[32,80,128]{2,1,0:T(8,128)(2,1)S(1)} async-done(((bf16[32,80,128]{2,1,0:T(8,128)(2,1)}), bf16[32,80,128]{2,1,0:T(8,128)(2,1)S(1)}, u32[]{:S(2)}, u32[]{:S(2)}) %all-to-all-start.3) | async-done | bytes 655392 | tf_op jit(solution)/shard_map/all_to_all | solution.py:58
  113.9 1.7 fusion.29
  115.6 0.5 fusion.96
  116.2 0.5 fusion.27
  116.6 0.5 fusion.13
  117.2 0.5 fusion.25
  117.6 0.5 fusion.17
  118.2 0.5 fusion.23
  118.6 0.5 fusion.18
  119.3 0.7 copy.95
  120.0 30.1 %all_to_all.31 = bf16[256,2,640]{2,1,0:T(2,128)(2,1)S(1)} all-to-all(bf16[256,2,640]{2,1,0:T(2,128)(2,1)S(1)} %copy.95), channel_id=1, replica_groups=mesh['sector'=32,'chan'=8] {'sector','chan'}, dimensions={0} | all-to-all | bytes 1310720 | tf_op jit(solution)/shard_map/all_to_all | solution.py:146
  150.1 0.5 reshape.275
  150.5 0.7 fusion.5
  151.2 1.1 copy.98
  152.3 5.6 %all-to-all-start.5 = ((bf16[32,80,128]{2,1,0:T(8,128)(2,1)}), bf16[32,80,128]{2,1,0:T(8,128)(2,1)S(1)}, u32[]{:S(2)}, u32[]{:S(2)}) async-start(bf16[32,80,128]{2,1,0:T(8,128)(2,1)} %bitcast.71), calls=%async_computation.5 | async-start | bytes 1310720 | tf_op jit(solution)/shard_map/all_to_all | solution.py:58
  157.9 3.5 %reshape.249 = bf16[5,8,16,2,640]{4,3,2,1,0:T(2,128)(2,1)S(1)} reshape(bf16[640,1280]{1,0:T(8,128)(2,1)} %all-gather.4.cloned.1.call-done) | data formatting | bytes 3276800 | tf_op jit(solution)/shard_map/reshape | solution.py:152
  161.4 16.5 %all-to-all-done.5 = bf16[32,80,128]{2,1,0:T(8,128)(2,1)S(1)} async-done(((bf16[32,80,128]{2,1,0:T(8,128)(2,1)}), bf16[32,80,128]{2,1,0:T(8,128)(2,1)S(1)}, u32[]{:S(2)}, u32[]{:S(2)}) %all-to-all-start.5) | async-done | bytes 655392 | tf_op jit(solution)/shard_map/all_to_all | solution.py:58
  177.9 0.8 fusion.14
  178.7 1.2 copy.101
  (63 shorter events, 3.3 us)
Async XLA Ops:
  6.5 1.1 copy-start
  6.5 13.7 %copy-start.2 = (bf16[128,2,640]{2,1,0:T(2,128)(2,1)S(1)}, bf16[128,2,640]{2,1,0:T(2,128)(2,1)}, u32[]{:S(2)}) copy-start(bf16[128,2,640]{2,1,0:T(2,128)(2,1)} %param.5) | copy-start | bytes 983044
  6.5 14.5 %copy-start.5 = (s32[16]{0:T(128)S(1)}, s32[16]{0:T(128)}, u32[]{:S(2)}) copy-start(s32[16]{0:T(128)} %param.6) | copy-start | bytes 196
  6.5 14.7 %copy-start.3 = (s32[2,2,16]{2,1,0:T(2,128)S(1)}, s32[2,2,16]{2,1,0:T(2,128)}, u32[]{:S(2)}) copy-start(s32[2,2,16]{2,1,0:T(2,128)} %param.7) | copy-start | bytes 772
  9.0 21.0 %all-to-all-start = ((bf16[32,15,128]{2,1,0:T(8,128)(2,1)}), bf16[32,15,128]{2,1,0:T(8,128)(2,1)S(1)}, u32[]{:S(2)}, u32[]{:S(2)}) async-start(bf16[32,15,128]{2,1,0:T(8,128)(2,1)} %copy.84), calls=%async_computation | async-start | bytes 262144 | tf_op jit(solution)/shard_map/all_to_all | solution.py:58
  20.2 40.6 %all-gather.6.cloned.1.call-start = ((), (), s32[]{:S(2)}) async-start(), calls=%async_computation.7 | async-start | bytes 2949120 | tf_op jit(solution)/shard_map/all_gather | solution.py:72
  21.0 92.9 %all-gather.8.cloned.1.call-start = ((), (), s32[]{:S(2)}) async-start(), calls=%async_computation.8 | async-start | bytes 3686400 | tf_op jit(solution)/shard_map/all_gather | solution.py:100
  60.8 9.8 %copy-start.4 = (f32[2,2,16,16]{3,2,1,0:T(8,128)S(1)}, f32[2,2,16,16]{3,2,1,0:T(8,128)}, u32[]{:S(2)}) copy-start(f32[2,2,16,16]{3,2,1,0:T(8,128)} %param.9) | copy-start | bytes 12292
  64.6 24.2 %all-to-all-start.2 = ((bf16[32,80,128]{2,1,0:T(8,128)(2,1)}), bf16[32,80,128]{2,1,0:T(8,128)(2,1)S(1)}, u32[]{:S(2)}, u32[]{:S(2)}) async-start(bf16[32,80,128]{2,1,0:T(8,128)(2,1)} %bitcast.40), calls=%async_computation.2 | async-start | bytes 1310720 | tf_op jit(solution)/shard_map/all_to_all | solution.py:58
  90.4 23.4 %all-to-all-start.3 = ((bf16[32,80,128]{2,1,0:T(8,128)(2,1)}), bf16[32,80,128]{2,1,0:T(8,128)(2,1)S(1)}, u32[]{:S(2)}, u32[]{:S(2)}) async-start(bf16[32,80,128]{2,1,0:T(8,128)(2,1)} %bitcast.51), calls=%async_computation.3 | async-start | bytes 1310720 | tf_op jit(solution)/shard_map/all_to_all | solution.py:58
  95.2 62.7 %all-gather.4.cloned.1.call-start = ((), (), s32[]{:S(2)}) async-start(), calls=%async_computation.6 | async-start | bytes 1843200 | tf_op jit(solution)/shard_map/all_gather | solution.py:101
  113.9 2.3 %copy-start.1 = (bf16[640,2560]{1,0:T(8,128)(2,1)S(1)}, bf16[640,2560]{1,0:T(8,128)(2,1)}, u32[]{:S(2)}) copy-start(bf16[640,2560]{1,0:T(8,128)(2,1)} %all-gather.8.cloned.1.call-done) | copy-start | bytes 9830404
  152.3 25.6 %all-to-all-start.5 = ((bf16[32,80,128]{2,1,0:T(8,128)(2,1)}), bf16[32,80,128]{2,1,0:T(8,128)(2,1)S(1)}, u32[]{:S(2)}, u32[]{:S(2)}) async-start(bf16[32,80,128]{2,1,0:T(8,128)(2,1)} %bitcast.71), calls=%async_computation.5 | async-start | bytes 1310720 | tf_op jit(solution)/shard_map/all_to_all | solution.py:58
Sparse Core Ops, SparseCore 0:
  22.8 29.7 all-gather.5
  60.5 27.2 all-gather.7
  100.0 28.1 all-gather.3

commit v6 on v5

--- a/solution.py
+++ b/solution.py
@@ -2,6 +2,7 @@
 import jax.numpy as jnp
 from jax import lax
 from jax.sharding import PartitionSpec as P
+
 
 TILE = 128
 NSEC = 16
@@ -97,7 +98,8 @@
     def rows_of(groups):
         return groups.transpose(1, 4, 2, 0, 3, 5).reshape(part, -1)
 
-    maps_a = lax.all_gather(rows_of(landed[:, :, 1:3]), "chan", axis=0, tiled=True)
+    laid = rows_of(landed[:, :, 1:3])
+    maps_a = lax.all_gather(laid, "chan", axis=0, tiled=True)
     maps_b = lax.all_gather(rows_of(landed[:, :, 3:4]), "chan", axis=0, tiled=True)
     slim = landed[:, :, 0].transpose(0, 2, 1, 3, 4).reshape(2 * MAXK * fine, window)
     column = jnp.arange(window, dtype=jnp.int32)
@@ -105,7 +107,8 @@
 
     first = jnp.einsum("dj,waj->wda", slim, gathered, preferred_element_type=F32).astype(BF16)
     first = first.reshape(2, CHANS, 2 * MAXK, fine, TILE).transpose(3, 0, 2, 1, 4)
-    first = deliver(first.reshape(tiles, 2 * MAXK * CHANS, TILE))
+    first = first.reshape(tiles, 2 * MAXK * CHANS, TILE)
+    first = deliver(first)
     select0 = selection(own[0], (anchor[0][0], anchor[1][0]), tiles)
     select1 = selection(own[0], (anchor[0][1], anchor[1][1]), tiles)
     first, select1 = lax.optimization_barrier((first, select1))

time: 187 us -> 187 us (level)
  no operation moved by 1% of the time
where the time goes in v6:
time: 187 us; the launch traced here: 186 us
  blocking collectives  57.5 us (31%)
  waiting for transfers between devices  55 us (29%)
  starting transfers between devices  26.9 us (14%)
  local copies, waits for them, and re-layouts  15.8 us (8%)
  matrix products  14.7 us (8%)
  between operations  14.2 us (8%)
  other arithmetic  2.41 us (1%)
    all_to_all x4, waiting for transfers between devices, deliver(): return lax.all_to_all(blocks, 'sector', 0, 0, tiled=True)  54.9 us
    all_to_all x1, blocking collectives, per_device(): fourth = lax.all_to_all(fourth, ('sector', 'chan'), 0, 0, tiled=True)  30.1 us
    all_to_all x1, blocking collectives, deliver(): return lax.all_to_all(blocks, 'sector', 0, 0, tiled=True)  27.4 us
    all_to_all x4, starting transfers between devices, deliver(): return lax.all_to_all(blocks, 'sector', 0, 0, tiled=True)  26.5 us
  transfers between devices with their start and end apart: 7, of which 4 were waited for; matrix products, arithmetic and copies ran while one was open for 15% of the time, Pallas kernels for 0%

profile of v6, /device:TPU:32, one launch (start us, length us, event | category | flops | bytes accessed | tf_op | source)
XLA Modules:
  0.0 186.4 jit_solution(11829165597034466676)
XLA Ops:
  6.5 1.1 copy-done
  8.3 0.7 copy.84
  9.0 11.2 %all-to-all-start = ((bf16[32,15,128]{2,1,0:T(8,128)(2,1)}), bf16[32,15,128]{2,1,0:T(8,128)(2,1)S(1)}, u32[]{:S(2)}, u32[]{:S(2)}) async-start(bf16[32,15,128]{2,1,0:T(8,128)(2,1)} %copy.84), calls=%async_computation | async-start | bytes 262144 | tf_op jit(solution)/shard_map/all_to_all | solution.py:59
  20.2 0.8 copy.140
  21.2 0.3 select_reduce_fusion.1
  22.1 0.6 select_reduce_fusion.12
  23.4 6.6 %all-to-all-done = bf16[32,15,128]{2,1,0:T(8,128)(2,1)S(1)} async-done(((bf16[32,15,128]{2,1,0:T(8,128)(2,1)}), bf16[32,15,128]{2,1,0:T(8,128)(2,1)S(1)}, u32[]{:S(2)}, u32[]{:S(2)}) %all-to-all-start) | async-done | bytes 122912 | tf_op jit(solution)/shard_map/all_to_all | solution.py:59
  30.0 0.3 fusion.20
  30.3 0.3 fusion.22
  31.0 0.3 copy.86
  31.4 27.4 %all_to_all.30 = bf16[32,100,128]{2,1,0:T(8,128)(2,1)S(1)} all-to-all(bf16[32,100,128]{2,1,0:T(8,128)(2,1)S(1)} %copy.86), channel_id=1, replica_groups=mesh['sector'=32,'chan'=8] {'sector'}, dimensions={0} | all-to-all | bytes 1638400 | tf_op jit(solution)/shard_map/all_to_all | solution.py:59
  59.1 1.2 reshape.256
  60.8 2.8 %convolution_convert_fusion = bf16[160,16,128]{2,0,1:T(8,128)(2,1)S(1)} fusion(bf16[16,128,640]{2,1,0:T(8,128)(2,1)} %all-gather.6.cloned.1.call-done, bf16[20,8,5,128]{3,2,1,0:T(8,128)(2,1)S(1)} %bitcast.197, pred[640]{0:T(1024)(128)(4,1)S(1)} %iota_compare_fusion.22), kind=kOutput, calls=%fused_computation.7 | convolution fusion | flops 419860480 | bytes 3482240 | tf_op jit(solution)/shard_map/dj,waj->wda/dot_general | solution.py:108
  63.5 1.1 copy.91
  64.6 5.0 %all-to-all-start.2 = ((bf16[32,80,128]{2,1,0:T(8,128)(2,1)}), bf16[32,80,128]{2,1,0:T(8,128)(2,1)S(1)}, u32[]{:S(2)}, u32[]{:S(2)}) async-start(bf16[32,80,128]{2,1,0:T(8,128)(2,1)} %bitcast.40), calls=%async_computation.2 | async-start | bytes 1310720 | tf_op jit(solution)/shard_map/all_to_all | solution.py:59
  70.0 0.6 fusion.95
  70.8 0.3 fusion.46
  71.0 17.8 %all-to-all-done.2 = bf16[32,80,128]{2,1,0:T(8,128)(2,1)S(1)} async-done(((bf16[32,80,128]{2,1,0:T(8,128)(2,1)}), bf16[32,80,128]{2,1,0:T(8,128)(2,1)S(1)}, u32[]{:S(2)}, u32[]{:S(2)}) %all-to-all-start.2) | async-done | bytes 655392 | tf_op jit(solution)/shard_map/all_to_all | solution.py:59
  88.8 0.5 fusion.6
  89.3 1.1 copy.93
  90.4 4.8 %all-to-all-start.3 = ((bf16[32,80,128]{2,1,0:T(8,128)(2,1)}), bf16[32,80,128]{2,1,0:T(8,128)(2,1)S(1)}, u32[]{:S(2)}, u32[]{:S(2)}) async-start(bf16[32,80,128]{2,1,0:T(8,128)(2,1)} %bitcast.51), calls=%async_computation.3 | async-start | bytes 1310720 | tf_op jit(solution)/shard_map/all_to_all | solution.py:59
  95.2 0.2 all-gather.4.cloned.1.call-start
  95.5 0.9 fusion.45
  96.4 0.9 fusion.44
  97.3 0.4 convolution_select_fusion.2
  97.7 0.4 convolution_select_fusion.1
  98.1 0.4 convolution_select_fusion.3
  98.5 0.4 convolution_select_fusion
  98.9 0.9 reshape.248
  99.9 14.0 %all-to-all-done.3 = bf16[32,80,128]{2,1,0:T(8,128)(2,1)S(1)} async-done(((bf16[32,80,128]{2,1,0:T(8,128)(2,1)}), bf16[32,80,128]{2,1,0:T(8,128)(2,1)S(1)}, u32[]{:S(2)}, u32[]{:S(2)}) %all-to-all-start.3) | async-done | bytes 655392 | tf_op jit(solution)/shard_map/all_to_all | solution.py:59
  113.9 1.7 fusion.29
  115.6 0.5 fusion.96
  116.2 0.5 fusion.27
  116.6 0.5 fusion.13
  117.2 0.5 fusion.25
  117.6 0.5 fusion.17
  118.2 0.5 fusion.23
  118.6 0.5 fusion.18
  119.3 0.7 copy.95
  120.0 30.1 %all_to_all.31 = bf16[256,2,640]{2,1,0:T(2,128)(2,1)S(1)} all-to-all(bf16[256,2,640]{2,1,0:T(2,128)(2,1)S(1)} %copy.95), channel_id=1, replica_groups=mesh['sector'=32,'chan'=8] {'sector','chan'}, dimensions={0} | all-to-all | bytes 1310720 | tf_op jit(solution)/shard_map/all_to_all | solution.py:149
  150.1 0.5 reshape.275
  150.5 0.7 fusion.5
  151.2 1.1 copy.98
  152.3 5.6 %all-to-all-start.5 = ((bf16[32,80,128]{2,1,0:T(8,128)(2,1)}), bf16[32,80,128]{2,1,0:T(8,128)(2,1)S(1)}, u32[]{:S(2)}, u32[]{:S(2)}) async-start(bf16[32,80,128]{2,1,0:T(8,128)(2,1)} %bitcast.71), calls=%async_computation.5 | async-start | bytes 1310720 | tf_op jit(solution)/shard_map/all_to_all | solution.py:59
  157.9 3.5 %reshape.249 = bf16[5,8,16,2,640]{4,3,2,1,0:T(2,128)(2,1)S(1)} reshape(bf16[640,1280]{1,0:T(8,128)(2,1)} %all-gather.4.cloned.1.call-done) | data formatting | bytes 3276800 | tf_op jit(solution)/shard_map/reshape | solution.py:155
  161.4 16.5 %all-to-all-done.5 = bf16[32,80,128]{2,1,0:T(8,128)(2,1)S(1)} async-done(((bf16[32,80,128]{2,1,0:T(8,128)(2,1)}), bf16[32,80,128]{2,1,0:T(8,128)(2,1)S(1)}, u32[]{:S(2)}, u32[]{:S(2)}) %all-to-all-start.5) | async-done | bytes 655392 | tf_op jit(solution)/shard_map/all_to_all | solution.py:59
  177.9 0.8 fusion.14
  178.7 1.2 copy.101
  (63 shorter events, 3.3 us)
Async XLA Ops:
  6.5 1.1 copy-start
  6.5 13.7 %copy-start.2 = (bf16[128,2,640]{2,1,0:T(2,128)(2,1)S(1)}, bf16[128,2,640]{2,1,0:T(2,128)(2,1)}, u32[]{:S(2)}) copy-start(bf16[128,2,640]{2,1,0:T(2,128)(2,1)} %param.5) | copy-start | bytes 983044
  6.5 14.5 %copy-start.5 = (s32[16]{0:T(128)S(1)}, s32[16]{0:T(128)}, u32[]{:S(2)}) copy-start(s32[16]{0:T(128)} %param.6) | copy-start | bytes 196
  6.5 14.7 %copy-start.3 = (s32[2,2,16]{2,1,0:T(2,128)S(1)}, s32[2,2,16]{2,1,0:T(2,128)}, u32[]{:S(2)}) copy-start(s32[2,2,16]{2,1,0:T(2,128)} %param.7) | copy-start | bytes 772
  9.0 21.0 %all-to-all-start = ((bf16[32,15,128]{2,1,0:T(8,128)(2,1)}), bf16[32,15,128]{2,1,0:T(8,128)(2,1)S(1)}, u32[]{:S(2)}, u32[]{:S(2)}) async-start(bf16[32,15,128]{2,1,0:T(8,128)(2,1)} %copy.84), calls=%async_computation | async-start | bytes 262144 | tf_op jit(solution)/shard_map/all_to_all | solution.py:59
  20.2 40.6 %all-gather.6.cloned.1.call-start = ((), (), s32[]{:S(2)}) async-start(), calls=%async_computation.7 | async-start | bytes 2949120 | tf_op jit(solution)/shard_map/all_gather | solution.py:73
  21.0 92.9 %all-gather.8.cloned.1.call-start = ((), (), s32[]{:S(2)}) async-start(), calls=%async_computation.8 | async-start | bytes 3686400 | tf_op jit(solution)/shard_map/all_gather | solution.py:102
  60.8 9.8 %copy-start.4 = (f32[2,2,16,16]{3,2,1,0:T(8,128)S(1)}, f32[2,2,16,16]{3,2,1,0:T(8,128)}, u32[]{:S(2)}) copy-start(f32[2,2,16,16]{3,2,1,0:T(8,128)} %param.9) | copy-start | bytes 12292
  64.6 24.2 %all-to-all-start.2 = ((bf16[32,80,128]{2,1,0:T(8,128)(2,1)}), bf16[32,80,128]{2,1,0:T(8,128)(2,1)S(1)}, u32[]{:S(2)}, u32[]{:S(2)}) async-start(bf16[32,80,128]{2,1,0:T(8,128)(2,1)} %bitcast.40), calls=%async_computation.2 | async-start | bytes 1310720 | tf_op jit(solution)/shard_map/all_to_all | solution.py:59
  90.4 23.4 %all-to-all-start.3 = ((bf16[32,80,128]{2,1,0:T(8,128)(2,1)}), bf16[32,80,128]{2,1,0:T(8,128)(2,1)S(1)}, u32[]{:S(2)}, u32[]{:S(2)}) async-start(bf16[32,80,128]{2,1,0:T(8,128)(2,1)} %bitcast.51), calls=%async_computation.3 | async-start | bytes 1310720 | tf_op jit(solution)/shard_map/all_to_all | solution.py:59
  95.2 62.7 %all-gather.4.cloned.1.call-start = ((), (), s32[]{:S(2)}) async-start(), calls=%async_computation.6 | async-start | bytes 1843200 | tf_op jit(solution)/shard_map/all_gather | solution.py:103
  113.9 2.3 %copy-start.1 = (bf16[640,2560]{1,0:T(8,128)(2,1)S(1)}, bf16[640,2560]{1,0:T(8,128)(2,1)}, u32[]{:S(2)}) copy-start(bf16[640,2560]{1,0:T(8,128)(2,1)} %all-gather.8.cloned.1.call-done) | copy-start | bytes 9830404
  152.3 25.6 %all-to-all-start.5 = ((bf16[32,80,128]{2,1,0:T(8,128)(2,1)}), bf16[32,80,128]{2,1,0:T(8,128)(2,1)S(1)}, u32[]{:S(2)}, u32[]{:S(2)}) async-start(bf16[32,80,128]{2,1,0:T(8,128)(2,1)} %bitcast.71), calls=%async_computation.5 | async-start | bytes 1310720 | tf_op jit(solution)/shard_map/all_to_all | solution.py:59
Sparse Core Ops, SparseCore 0:
  22.8 29.7 all-gather.5
  60.5 27.2 all-gather.7
  100.0 28.1 all-gather.3

commit v7 on v6

--- a/solution.py
+++ b/solution.py
@@ -95,6 +95,8 @@
     landed = deliver(routed.reshape(tiles, 4 * MAXK * piece, TILE))
     landed = landed.reshape(2, half, 4, MAXK, piece, TILE)
 
+    landed, width, own_start, anchor = lax.optimization_barrier((landed, width, own[0], anchor))
+
     def rows_of(groups):
         return groups.transpose(1, 4, 2, 0, 3, 5).reshape(part, -1)
 
@@ -109,8 +111,8 @@
     first = first.reshape(2, CHANS, 2 * MAXK, fine, TILE).transpose(3, 0, 2, 1, 4)
     first = first.reshape(tiles, 2 * MAXK * CHANS, TILE)
     first = deliver(first)
-    select0 = selection(own[0], (anchor[0][0], anchor[1][0]), tiles)
-    select1 = selection(own[0], (anchor[0][1], anchor[1][1]), tiles)
+    select0 = selection(own_start, (anchor[0][0], anchor[1][0]), tiles)
+    select1 = selection(own_start, (anchor[0][1], anchor[1][1]), tiles)
     first, select1 = lax.optimization_barrier((first, select1))
     first = route(select0, first.reshape(tiles, 2, MAXK, CHANS, TILE))
     first = deliver(first.reshape(tiles, 2 * MAXK * CHANS, TILE))

time: 187 us -> 189 us (1.011)
  no operation moved by 1% of the time
where the time goes in v7:
time: 189 us; the launch traced here: 188 us
  blocking collectives  57.5 us (30%)
  waiting for transfers between devices  56.7 us (30%)
  starting transfers between devices  26.9 us (14%)
  local copies, waits for them, and re-layouts  15.8 us (8%)
  matrix products  14.6 us (8%)
  between operations  14.2 us (8%)
  other arithmetic  2.41 us (1%)
    all_to_all x4, waiting for transfers between devices, deliver(): return lax.all_to_all(blocks, 'sector', 0, 0, tiled=True)  56.6 us
    all_to_all x1, blocking collectives, per_device(): fourth = lax.all_to_all(fourth, ('sector', 'chan'), 0, 0, tiled=True)  30.1 us
    all_to_all x1, blocking collectives, deliver(): return lax.all_to_all(blocks, 'sector', 0, 0, tiled=True)  27.4 us
    all_to_all x4, starting transfers between devices, deliver(): return lax.all_to_all(blocks, 'sector', 0, 0, tiled=True)  26.6 us
  transfers between devices with their start and end apart: 7, of which 4 were waited for; matrix products, arithmetic and copies ran while one was open for 15% of the time, Pallas kernels for 0%

profile of v7, /device:TPU:32, one launch (start us, length us, event | category | flops | bytes accessed | tf_op | source)
XLA Modules:
  0.0 188.2 jit_solution(4064743551027960385)
XLA Ops:
  6.5 1.1 copy-done
  8.3 0.7 copy.84
  9.0 11.2 %all-to-all-start = ((bf16[32,15,128]{2,1,0:T(8,128)(2,1)}), bf16[32,15,128]{2,1,0:T(8,128)(2,1)S(1)}, u32[]{:S(2)}, u32[]{:S(2)}) async-start(bf16[32,15,128]{2,1,0:T(8,128)(2,1)} %copy.84), calls=%async_computation | async-start | bytes 262144 | tf_op jit(solution)/shard_map/all_to_all | solution.py:59
  20.2 0.8 copy.140
  21.2 0.3 select_reduce_fusion.1
  22.1 0.6 select_reduce_fusion.11
  23.4 6.6 %all-to-all-done = bf16[32,15,128]{2,1,0:T(8,128)(2,1)S(1)} async-done(((bf16[32,15,128]{2,1,0:T(8,128)(2,1)}), bf16[32,15,128]{2,1,0:T(8,128)(2,1)S(1)}, u32[]{:S(2)}, u32[]{:S(2)}) %all-to-all-start) | async-done | bytes 122912 | tf_op jit(solution)/shard_map/all_to_all | solution.py:59
  30.0 0.3 fusion.20
  30.3 0.3 fusion.22
  31.0 0.3 copy.86
  31.4 27.4 %all_to_all.30 = bf16[32,100,128]{2,1,0:T(8,128)(2,1)S(1)} all-to-all(bf16[32,100,128]{2,1,0:T(8,128)(2,1)S(1)} %copy.86), channel_id=1, replica_groups=mesh['sector'=32,'chan'=8] {'sector'}, dimensions={0} | all-to-all | bytes 1638400 | tf_op jit(solution)/shard_map/all_to_all | solution.py:59
  59.1 1.2 reshape.250
  60.4 0.6 fusion.97
  61.0 0.8 fusion.45
  61.9 0.4 convolution_select_fusion.2
  62.5 2.7 %convolution_convert_fusion = bf16[160,16,128]{2,0,1:T(8,128)(2,1)S(1)} fusion(bf16[16,128,640]{2,1,0:T(8,128)(2,1)} %all-gather.6.cloned.1.call-done, bf16[20,8,5,128]{3,2,1,0:T(8,128)(2,1)S(1)} %bitcast.201, pred[640]{0:T(1024)(128)(4,1)S(1)} %iota_compare_fusion.22), kind=kOutput, calls=%fused_computation.7 | convolution fusion | flops 419860480 | bytes 3482240 | tf_op jit(solution)/shard_map/dj,waj->wda/dot_general | solution.py:110
  65.3 1.1 copy.91
  66.4 5.0 %all-to-all-start.2 = ((bf16[32,80,128]{2,1,0:T(8,128)(2,1)}), bf16[32,80,128]{2,1,0:T(8,128)(2,1)S(1)}, u32[]{:S(2)}, u32[]{:S(2)}) async-start(bf16[32,80,128]{2,1,0:T(8,128)(2,1)} %bitcast.40), calls=%async_computation.2 | async-start | bytes 1310720 | tf_op jit(solution)/shard_map/all_to_all | solution.py:59
  71.8 18.8 %all-to-all-done.2 = bf16[32,80,128]{2,1,0:T(8,128)(2,1)S(1)} async-done(((bf16[32,80,128]{2,1,0:T(8,128)(2,1)}), bf16[32,80,128]{2,1,0:T(8,128)(2,1)S(1)}, u32[]{:S(2)}, u32[]{:S(2)}) %all-to-all-start.2) | async-done | bytes 655392 | tf_op jit(solution)/shard_map/all_to_all | solution.py:59
  90.6 0.5 fusion.6
  91.0 1.1 copy.93
  92.1 4.8 %all-to-all-start.3 = ((bf16[32,80,128]{2,1,0:T(8,128)(2,1)}), bf16[32,80,128]{2,1,0:T(8,128)(2,1)S(1)}, u32[]{:S(2)}, u32[]{:S(2)}) async-start(bf16[32,80,128]{2,1,0:T(8,128)(2,1)} %bitcast.52), calls=%async_computation.3 | async-start | bytes 1310720 | tf_op jit(solution)/shard_map/all_to_all | solution.py:59
  97.0 0.2 all-gather.4.cloned.1.call-start
  97.2 0.8 fusion.44
  98.0 0.4 convolution_select_fusion.1
  98.6 0.9 reshape.242
  99.8 0.3 fusion.46
  100.0 0.4 convolution_select_fusion.3
  100.5 0.4 convolution_select_fusion
  100.8 14.8 %all-to-all-done.3 = bf16[32,80,128]{2,1,0:T(8,128)(2,1)S(1)} async-done(((bf16[32,80,128]{2,1,0:T(8,128)(2,1)}), bf16[32,80,128]{2,1,0:T(8,128)(2,1)S(1)}, u32[]{:S(2)}, u32[]{:S(2)}) %all-to-all-start.3) | async-done | bytes 655392 | tf_op jit(solution)/shard_map/all_to_all | solution.py:59
  115.6 1.8 fusion.29
  117.3 0.5 fusion.98
  117.9 0.5 fusion.27
  118.4 0.5 fusion.13
  118.9 0.5 fusion.25
  119.4 0.5 fusion.17
  119.9 0.5 fusion.23
  120.4 0.5 fusion.18
  121.0 0.7 copy.95
  121.7 30.1 %all_to_all.31 = bf16[256,2,640]{2,1,0:T(2,128)(2,1)S(1)} all-to-all(bf16[256,2,640]{2,1,0:T(2,128)(2,1)S(1)} %copy.95), channel_id=1, replica_groups=mesh['sector'=32,'chan'=8] {'sector','chan'}, dimensions={0} | all-to-all | bytes 1310720 | tf_op jit(solution)/shard_map/all_to_all | solution.py:151
  151.8 0.5 reshape.269
  152.3 0.7 fusion.5
  153.0 1.1 copy.98
  154.1 5.6 %all-to-all-start.5 = ((bf16[32,80,128]{2,1,0:T(8,128)(2,1)}), bf16[32,80,128]{2,1,0:T(8,128)(2,1)S(1)}, u32[]{:S(2)}, u32[]{:S(2)}) async-start(bf16[32,80,128]{2,1,0:T(8,128)(2,1)} %bitcast.72), calls=%async_computation.5 | async-start | bytes 1310720 | tf_op jit(solution)/shard_map/all_to_all | solution.py:59
  159.7 3.5 %reshape.243 = bf16[5,8,16,2,640]{4,3,2,1,0:T(2,128)(2,1)S(1)} reshape(bf16[640,1280]{1,0:T(8,128)(2,1)} %all-gather.4.cloned.1.call-done) | data formatting | bytes 3276800 | tf_op jit(solution)/shard_map/reshape | solution.py:157
  163.2 16.5 %all-to-all-done.5 = bf16[32,80,128]{2,1,0:T(8,128)(2,1)S(1)} async-done(((bf16[32,80,128]{2,1,0:T(8,128)(2,1)}), bf16[32,80,128]{2,1,0:T(8,128)(2,1)S(1)}, u32[]{:S(2)}, u32[]{:S(2)}) %all-to-all-start.5) | async-done | bytes 655392 | tf_op jit(solution)/shard_map/all_to_all | solution.py:59
  179.6 0.8 fusion.14
  180.5 1.2 copy.101
  (63 shorter events, 3.3 us)
Async XLA Ops:
  6.5 1.1 copy-start
  6.5 13.7 %copy-start.2 = (bf16[128,2,640]{2,1,0:T(2,128)(2,1)S(1)}, bf16[128,2,640]{2,1,0:T(2,128)(2,1)}, u32[]{:S(2)}) copy-start(bf16[128,2,640]{2,1,0:T(2,128)(2,1)} %param.5) | copy-start | bytes 983044
  6.5 14.5 %copy-start.5 = (s32[16]{0:T(128)S(1)}, s32[16]{0:T(128)}, u32[]{:S(2)}) copy-start(s32[16]{0:T(128)} %param.6) | copy-start | bytes 196
  6.5 14.7 %copy-start.3 = (s32[2,2,16]{2,1,0:T(2,128)S(1)}, s32[2,2,16]{2,1,0:T(2,128)}, u32[]{:S(2)}) copy-start(s32[2,2,16]{2,1,0:T(2,128)} %param.7) | copy-start | bytes 772
  9.0 21.0 %all-to-all-start = ((bf16[32,15,128]{2,1,0:T(8,128)(2,1)}), bf16[32,15,128]{2,1,0:T(8,128)(2,1)S(1)}, u32[]{:S(2)}, u32[]{:S(2)}) async-start(bf16[32,15,128]{2,1,0:T(8,128)(2,1)} %copy.84), calls=%async_computation | async-start | bytes 262144 | tf_op jit(solution)/shard_map/all_to_all | solution.py:59
  20.2 42.3 %all-gather.6.cloned.1.call-start = ((), (), s32[]{:S(2)}) async-start(), calls=%async_computation.7 | async-start | bytes 2949120 | tf_op jit(solution)/shard_map/all_gather | solution.py:73
  21.0 94.6 %all-gather.8.cloned.1.call-start = ((), (), s32[]{:S(2)}) async-start(), calls=%async_computation.8 | async-start | bytes 3686400 | tf_op jit(solution)/shard_map/all_gather | solution.py:104
  58.7 2.3 %copy-start.4 = (f32[2,2,16,16]{3,2,1,0:T(8,128)S(1)}, f32[2,2,16,16]{3,2,1,0:T(8,128)}, u32[]{:S(2)}) copy-start(f32[2,2,16,16]{3,2,1,0:T(8,128)} %param.9) | copy-start | bytes 12292
  66.4 24.2 %all-to-all-start.2 = ((bf16[32,80,128]{2,1,0:T(8,128)(2,1)}), bf16[32,80,128]{2,1,0:T(8,128)(2,1)S(1)}, u32[]{:S(2)}, u32[]{:S(2)}) async-start(bf16[32,80,128]{2,1,0:T(8,128)(2,1)} %bitcast.40), calls=%async_computation.2 | async-start | bytes 1310720 | tf_op jit(solution)/shard_map/all_to_all | solution.py:59
  92.1 23.4 %all-to-all-start.3 = ((bf16[32,80,128]{2,1,0:T(8,128)(2,1)}), bf16[32,80,128]{2,1,0:T(8,128)(2,1)S(1)}, u32[]{:S(2)}, u32[]{:S(2)}) async-start(bf16[32,80,128]{2,1,0:T(8,128)(2,1)} %bitcast.52), calls=%async_computation.3 | async-start | bytes 1310720 | tf_op jit(solution)/shard_map/all_to_all | solution.py:59
  97.0 62.7 %all-gather.4.cloned.1.call-start = ((), (), s32[]{:S(2)}) async-start(), calls=%async_computation.6 | async-start | bytes 1843200 | tf_op jit(solution)/shard_map/all_gather | solution.py:105
  115.6 2.3 %copy-start.1 = (bf16[640,2560]{1,0:T(8,128)(2,1)S(1)}, bf16[640,2560]{1,0:T(8,128)(2,1)}, u32[]{:S(2)}) copy-start(bf16[640,2560]{1,0:T(8,128)(2,1)} %all-gather.8.cloned.1.call-done) | copy-start | bytes 9830404
  154.1 25.6 %all-to-all-start.5 = ((bf16[32,80,128]{2,1,0:T(8,128)(2,1)}), bf16[32,80,128]{2,1,0:T(8,128)(2,1)S(1)}, u32[]{:S(2)}, u32[]{:S(2)}) async-start(bf16[32,80,128]{2,1,0:T(8,128)(2,1)} %bitcast.72), calls=%async_computation.5 | async-start | bytes 1310720 | tf_op jit(solution)/shard_map/all_to_all | solution.py:59
Sparse Core Ops, SparseCore 0:
  22.8 29.7 all-gather.5
  60.5 27.2 all-gather.7
  99.7 28.2 all-gather.3

commit v8 on v7

--- a/solution.py
+++ b/solution.py
@@ -102,7 +102,8 @@
 
     laid = rows_of(landed[:, :, 1:3])
     maps_a = lax.all_gather(laid, "chan", axis=0, tiled=True)
-    maps_b = lax.all_gather(rows_of(landed[:, :, 3:4]), "chan", axis=0, tiled=True)
+    laid = rows_of(landed[:, :, 3:4])
+    maps_b = lax.all_gather(laid, "chan", axis=0, tiled=True)
     slim = landed[:, :, 0].transpose(0, 2, 1, 3, 4).reshape(2 * MAXK * fine, window)
     column = jnp.arange(window, dtype=jnp.int32)
     slim = jnp.where(column < width, slim, jnp.zeros((), BF16))
@@ -133,12 +134,14 @@
 
     scale0 = 3.0 / anchor_width.astype(F32)
     scale1 = 3.0 / width.astype(F32)
+    blends = [blend(mixing[0, s] * scale0[s], natural) for s in range(2)]
+    blends += [blend(mixing[1, s] * scale1, paired) for s in range(2)]
     mixed = jnp.zeros((tiles * CHANS, window), F32)
     for s in range(2):
         second = jnp.dot(
             rows[s], maps_a[:, s * window : (s + 1) * window], preferred_element_type=F32
         )
-        mixed = mixed + jnp.dot(blend(mixing[0, s] * scale0[s], natural), second, precision=fast)
+        mixed = mixed + jnp.dot(blends[s], second, precision=fast)
     middle = mixed.astype(BF16)
 
     fourth = []
@@ -146,7 +149,7 @@
         third = jnp.dot(
             middle, maps_a[:, s * window : (s + 1) * window], preferred_element_type=F32
         )
-        fourth.append(jnp.dot(blend(mixing[1, s - 2] * scale1, paired), third, precision=fast))
+        fourth.append(jnp.dot(blends[s], third, precision=fast))
     fourth = jnp.stack(fourth, axis=1).astype(BF16)
     fourth = lax.all_to_all(fourth, ("sector", "chan"), 0, 0, tiled=True)
     fourth = fourth.reshape(tiles, CHANS, 2, MAXK, TILE).transpose(0, 2, 3, 1, 4)

time: 189 us -> 189 us (level)
  no operation moved by 1% of the time
where the time goes in v8:
time: 189 us; the launch traced here: 188 us
  blocking collectives  57.5 us (30%)
  waiting for transfers between devices  56.7 us (30%)
  starting transfers between devices  26.9 us (14%)
  local copies, waits for them, and re-layouts  15.8 us (8%)
  matrix products  14.6 us (8%)
  between operations  14.2 us (8%)
  other arithmetic  2.41 us (1%)
    all_to_all x4, waiting for transfers between devices, deliver(): return lax.all_to_all(blocks, 'sector', 0, 0, tiled=True)  56.6 us
    all_to_all x1, blocking collectives, per_device(): fourth = lax.all_to_all(fourth, ('sector', 'chan'), 0, 0, tiled=True)  30.1 us
    all_to_all x1, blocking collectives, deliver(): return lax.all_to_all(blocks, 'sector', 0, 0, tiled=True)  27.4 us
    all_to_all x4, starting transfers between devices, deliver(): return lax.all_to_all(blocks, 'sector', 0, 0, tiled=True)  26.6 us
  transfers between devices with their start and end apart: 7, of which 4 were waited for; matrix products, arithmetic and copies ran while one was open for 15% of the time, Pallas kernels for 0%

profile of v8, /device:TPU:32, one launch (start us, length us, event | category | flops | bytes accessed | tf_op | source)
XLA Modules:
  0.0 188.2 jit_solution(4064743551027960385)
XLA Ops:
  6.5 1.1 copy-done
  8.3 0.7 copy.84
  9.0 11.2 %all-to-all-start = ((bf16[32,15,128]{2,1,0:T(8,128)(2,1)}), bf16[32,15,128]{2,1,0:T(8,128)(2,1)S(1)}, u32[]{:S(2)}, u32[]{:S(2)}) async-start(bf16[32,15,128]{2,1,0:T(8,128)(2,1)} %copy.84), calls=%async_computation | async-start | bytes 262144 | tf_op jit(solution)/shard_map/all_to_all | solution.py:59
  20.2 0.8 copy.140
  21.2 0.3 select_reduce_fusion.1
  22.1 0.6 select_reduce_fusion.11
  23.4 6.6 %all-to-all-done = bf16[32,15,128]{2,1,0:T(8,128)(2,1)S(1)} async-done(((bf16[32,15,128]{2,1,0:T(8,128)(2,1)}), bf16[32,15,128]{2,1,0:T(8,128)(2,1)S(1)}, u32[]{:S(2)}, u32[]{:S(2)}) %all-to-all-start) | async-done | bytes 122912 | tf_op jit(solution)/shard_map/all_to_all | solution.py:59
  30.0 0.3 fusion.20
  30.3 0.3 fusion.22
  31.0 0.3 copy.86
  31.4 27.4 %all_to_all.30 = bf16[32,100,128]{2,1,0:T(8,128)(2,1)S(1)} all-to-all(bf16[32,100,128]{2,1,0:T(8,128)(2,1)S(1)} %copy.86), channel_id=1, replica_groups=mesh['sector'=32,'chan'=8] {'sector'}, dimensions={0} | all-to-all | bytes 1638400 | tf_op jit(solution)/shard_map/all_to_all | solution.py:59
  59.1 1.2 reshape.250
  60.4 0.6 fusion.97
  61.0 0.8 fusion.45
  61.9 0.4 convolution_select_fusion.2
  62.5 2.7 %convolution_convert_fusion = bf16[160,16,128]{2,0,1:T(8,128)(2,1)S(1)} fusion(bf16[16,128,640]{2,1,0:T(8,128)(2,1)} %all-gather.6.cloned.1.call-done, bf16[20,8,5,128]{3,2,1,0:T(8,128)(2,1)S(1)} %bitcast.201, pred[640]{0:T(1024)(128)(4,1)S(1)} %iota_compare_fusion.22), kind=kOutput, calls=%fused_computation.7 | convolution fusion | flops 419860480 | bytes 3482240 | tf_op jit(solution)/shard_map/dj,waj->wda/dot_general | solution.py:111
  65.3 1.1 copy.91
  66.4 5.0 %all-to-all-start.2 = ((bf16[32,80,128]{2,1,0:T(8,128)(2,1)}), bf16[32,80,128]{2,1,0:T(8,128)(2,1)S(1)}, u32[]{:S(2)}, u32[]{:S(2)}) async-start(bf16[32,80,128]{2,1,0:T(8,128)(2,1)} %bitcast.40), calls=%async_computation.2 | async-start | bytes 1310720 | tf_op jit(solution)/shard_map/all_to_all | solution.py:59
  71.8 18.8 %all-to-all-done.2 = bf16[32,80,128]{2,1,0:T(8,128)(2,1)S(1)} async-done(((bf16[32,80,128]{2,1,0:T(8,128)(2,1)}), bf16[32,80,128]{2,1,0:T(8,128)(2,1)S(1)}, u32[]{:S(2)}, u32[]{:S(2)}) %all-to-all-start.2) | async-done | bytes 655392 | tf_op jit(solution)/shard_map/all_to_all | solution.py:59
  90.6 0.5 fusion.6
  91.0 1.1 copy.93
  92.1 4.8 %all-to-all-start.3 = ((bf16[32,80,128]{2,1,0:T(8,128)(2,1)}), bf16[32,80,128]{2,1,0:T(8,128)(2,1)S(1)}, u32[]{:S(2)}, u32[]{:S(2)}) async-start(bf16[32,80,128]{2,1,0:T(8,128)(2,1)} %bitcast.52), calls=%async_computation.3 | async-start | bytes 1310720 | tf_op jit(solution)/shard_map/all_to_all | solution.py:59
  97.0 0.2 all-gather.4.cloned.1.call-start
  97.2 0.8 fusion.44
  98.0 0.4 convolution_select_fusion.1
  98.6 0.9 reshape.242
  99.8 0.3 fusion.46
  100.0 0.4 convolution_select_fusion.3
  100.5 0.4 convolution_select_fusion
  100.8 14.8 %all-to-all-done.3 = bf16[32,80,128]{2,1,0:T(8,128)(2,1)S(1)} async-done(((bf16[32,80,128]{2,1,0:T(8,128)(2,1)}), bf16[32,80,128]{2,1,0:T(8,128)(2,1)S(1)}, u32[]{:S(2)}, u32[]{:S(2)}) %all-to-all-start.3) | async-done | bytes 655392 | tf_op jit(solution)/shard_map/all_to_all | solution.py:59
  115.6 1.8 fusion.29
  117.3 0.5 fusion.98
  117.9 0.5 fusion.27
  118.4 0.5 fusion.13
  118.9 0.5 fusion.25
  119.4 0.5 fusion.17
  119.9 0.5 fusion.23
  120.4 0.5 fusion.18
  121.0 0.7 copy.95
  121.7 30.1 %all_to_all.31 = bf16[256,2,640]{2,1,0:T(2,128)(2,1)S(1)} all-to-all(bf16[256,2,640]{2,1,0:T(2,128)(2,1)S(1)} %copy.95), channel_id=1, replica_groups=mesh['sector'=32,'chan'=8] {'sector','chan'}, dimensions={0} | all-to-all | bytes 1310720 | tf_op jit(solution)/shard_map/all_to_all | solution.py:154
  151.8 0.5 reshape.269
  152.3 0.7 fusion.5
  153.0 1.1 copy.98
  154.1 5.6 %all-to-all-start.5 = ((bf16[32,80,128]{2,1,0:T(8,128)(2,1)}), bf16[32,80,128]{2,1,0:T(8,128)(2,1)S(1)}, u32[]{:S(2)}, u32[]{:S(2)}) async-start(bf16[32,80,128]{2,1,0:T(8,128)(2,1)} %bitcast.72), calls=%async_computation.5 | async-start | bytes 1310720 | tf_op jit(solution)/shard_map/all_to_all | solution.py:59
  159.7 3.5 %reshape.243 = bf16[5,8,16,2,640]{4,3,2,1,0:T(2,128)(2,1)S(1)} reshape(bf16[640,1280]{1,0:T(8,128)(2,1)} %all-gather.4.cloned.1.call-done) | data formatting | bytes 3276800 | tf_op jit(solution)/shard_map/reshape | solution.py:160
  163.2 16.5 %all-to-all-done.5 = bf16[32,80,128]{2,1,0:T(8,128)(2,1)S(1)} async-done(((bf16[32,80,128]{2,1,0:T(8,128)(2,1)}), bf16[32,80,128]{2,1,0:T(8,128)(2,1)S(1)}, u32[]{:S(2)}, u32[]{:S(2)}) %all-to-all-start.5) | async-done | bytes 655392 | tf_op jit(solution)/shard_map/all_to_all | solution.py:59
  179.6 0.8 fusion.14
  180.5 1.2 copy.101
  (63 shorter events, 3.3 us)
Async XLA Ops:
  6.5 1.1 copy-start
  6.5 13.7 %copy-start.2 = (bf16[128,2,640]{2,1,0:T(2,128)(2,1)S(1)}, bf16[128,2,640]{2,1,0:T(2,128)(2,1)}, u32[]{:S(2)}) copy-start(bf16[128,2,640]{2,1,0:T(2,128)(2,1)} %param.5) | copy-start | bytes 983044
  6.5 14.5 %copy-start.5 = (s32[16]{0:T(128)S(1)}, s32[16]{0:T(128)}, u32[]{:S(2)}) copy-start(s32[16]{0:T(128)} %param.6) | copy-start | bytes 196
  6.5 14.7 %copy-start.3 = (s32[2,2,16]{2,1,0:T(2,128)S(1)}, s32[2,2,16]{2,1,0:T(2,128)}, u32[]{:S(2)}) copy-start(s32[2,2,16]{2,1,0:T(2,128)} %param.7) | copy-start | bytes 772
  9.0 21.0 %all-to-all-start = ((bf16[32,15,128]{2,1,0:T(8,128)(2,1)}), bf16[32,15,128]{2,1,0:T(8,128)(2,1)S(1)}, u32[]{:S(2)}, u32[]{:S(2)}) async-start(bf16[32,15,128]{2,1,0:T(8,128)(2,1)} %copy.84), calls=%async_computation | async-start | bytes 262144 | tf_op jit(solution)/shard_map/all_to_all | solution.py:59
  20.2 42.3 %all-gather.6.cloned.1.call-start = ((), (), s32[]{:S(2)}) async-start(), calls=%async_computation.7 | async-start | bytes 2949120 | tf_op jit(solution)/shard_map/all_gather | solution.py:73
  21.0 94.6 %all-gather.8.cloned.1.call-start = ((), (), s32[]{:S(2)}) async-start(), calls=%async_computation.8 | async-start | bytes 3686400 | tf_op jit(solution)/shard_map/all_gather | solution.py:104
  58.7 2.3 %copy-start.4 = (f32[2,2,16,16]{3,2,1,0:T(8,128)S(1)}, f32[2,2,16,16]{3,2,1,0:T(8,128)}, u32[]{:S(2)}) copy-start(f32[2,2,16,16]{3,2,1,0:T(8,128)} %param.9) | copy-start | bytes 12292
  66.4 24.2 %all-to-all-start.2 = ((bf16[32,80,128]{2,1,0:T(8,128)(2,1)}), bf16[32,80,128]{2,1,0:T(8,128)(2,1)S(1)}, u32[]{:S(2)}, u32[]{:S(2)}) async-start(bf16[32,80,128]{2,1,0:T(8,128)(2,1)} %bitcast.40), calls=%async_computation.2 | async-start | bytes 1310720 | tf_op jit(solution)/shard_map/all_to_all | solution.py:59
  92.1 23.4 %all-to-all-start.3 = ((bf16[32,80,128]{2,1,0:T(8,128)(2,1)}), bf16[32,80,128]{2,1,0:T(8,128)(2,1)S(1)}, u32[]{:S(2)}, u32[]{:S(2)}) async-start(bf16[32,80,128]{2,1,0:T(8,128)(2,1)} %bitcast.52), calls=%async_computation.3 | async-start | bytes 1310720 | tf_op jit(solution)/shard_map/all_to_all | solution.py:59
  97.0 62.7 %all-gather.4.cloned.1.call-start = ((), (), s32[]{:S(2)}) async-start(), calls=%async_computation.6 | async-start | bytes 1843200 | tf_op jit(solution)/shard_map/all_gather | solution.py:106
  115.6 2.3 %copy-start.1 = (bf16[640,2560]{1,0:T(8,128)(2,1)S(1)}, bf16[640,2560]{1,0:T(8,128)(2,1)}, u32[]{:S(2)}) copy-start(bf16[640,2560]{1,0:T(8,128)(2,1)} %all-gather.8.cloned.1.call-done) | copy-start | bytes 9830404
  154.1 25.6 %all-to-all-start.5 = ((bf16[32,80,128]{2,1,0:T(8,128)(2,1)}), bf16[32,80,128]{2,1,0:T(8,128)(2,1)S(1)}, u32[]{:S(2)}, u32[]{:S(2)}) async-start(bf16[32,80,128]{2,1,0:T(8,128)(2,1)} %bitcast.72), calls=%async_computation.5 | async-start | bytes 1310720 | tf_op jit(solution)/shard_map/all_to_all | solution.py:59
Sparse Core Ops, SparseCore 0:
  22.8 29.7 all-gather.5
  60.5 27.2 all-gather.7
  99.7 28.2 all-gather.3
